TPU v7x, 128 devices: a whole 4x4x4 slice. The times are simulated.
128 devices in a mesh: offset: 4 (over x), mid: 8 (over z, core), tm: 4 (over y).
Axes of the slice: x: 4, y: 4, z: 4, core: 2. Of those that a mesh axis runs over, the one named last changes fastest.
Arguments:
- traces: bfloat16 [32768, 1024], P(('offset', 'mid'), 'tm'), may hold values from -6 to 6
- dest: int32 [32768, 1], P(('offset', 'mid')), may hold values from 0 to 31; in each aligned block of 1024 rows (0 to 1023, 1024 to 2047, ...) at most 64 rows name the same one
- cell: int32 [32768, 1], P(('offset', 'mid')), may hold values from 0 to 511
- w_first: bfloat16 [16, 9], replicated, may hold values from -2 to 2
- w_mid: bfloat16 [2, 16, 144], replicated, may hold values from -0.5 to 0.5
- w_last: bfloat16 [1, 144], replicated, may hold values from -0.5 to 0.5
- bias: float32 [3, 16], replicated, may hold values from -3 to 3
Outputs:
- denoised: float32 [32, 512, 1024], P('offset', 'mid', 'tm')
Inputs may be any that keep to these rules, and one draw needn't show every extreme that they name: `dest`: among the traces of one device no owner is named more than 64 times, a bound that some block reaches.
All inputs are finite; a program needn't handle non-finite values.
Results may differ from a plain program's by a relative error of at most 0.0038.
Values may be sent and summed in bfloat16 or wider, within the bound.
No kernel may reach another device: no remote copies, remote signals or barrier semaphores. Data moves between devices by JAX's collectives and lax.ppermute only.
A program may use at most 256 MiB of HBM per device.

v0:
```python
import functools

import jax
import jax.numpy as jnp
from jax import lax
from jax.experimental import pallas as pl
from jax.experimental.pallas import tpu as pltpu
from jax.sharding import PartitionSpec as P

BF = jnp.bfloat16
F32 = jnp.float32
OWNERS = 32
SLOTS = 64
COUNT = 1024
TS = 256
CL = 8
MB = 64
HALO = 8
SEG = TS + 2 * HALO
LANES = CL * SEG
TILE = 128
TILES = 17
CHUNK = 2 * TILE
NCHUNK = 9
WIDE = CHUNK * NCHUNK
LEAD = 4
EXT = (LEAD + 22) * TILE
CH = 16
R1, R2, R3 = 78, 74, 66
TAPS = 240
KDIM = 256
GROUP = 3
EXTRA = 8
PAY = SLOTS + EXTRA


def slots_of(rows, groups):
    return [r for g in range(groups) for r in range(g, rows, groups)]


ORDER1 = slots_of(R1, 2)
ORDER2 = slots_of(R2, 4)
SLOT2 = {r: s for s, r in enumerate(ORDER2)}


def iota(shape, dim):
    return lax.broadcasted_iota(jnp.int32, shape, dim)


def onehot(mask):
    return jnp.where(mask, 1.0, 0.0).astype(BF)


def dot(a, b):
    return jnp.dot(a, b, preferred_element_type=F32)


def dot_t(a, b):
    return lax.dot_general(a, b, (((1,), (1,)), ((), ())), preferred_element_type=F32)


def send_kernel(dest_ref, cell_ref, traces_ref, out_hbm, token_ref, out_ref, sems):
    dest = dest_ref[...]
    cell = cell_ref[...]
    width = 256
    blocks = COUNT // width
    owner = iota((OWNERS, width), 0)
    hots = [owner == dest[:, n * width : (n + 1) * width] for n in range(blocks)]
    upper = onehot(iota((width, width), 0) < iota((width, width), 1))
    before = dot(jnp.concatenate([onehot(hot) for hot in hots], axis=0), upper)
    ranks = []
    offset = jnp.zeros((OWNERS, 1), F32)
    for n, hot in enumerate(hots):
        part = before[n * OWNERS : (n + 1) * OWNERS]
        ranks.append(jnp.sum(jnp.where(hot, part + offset, 0.0), axis=0, keepdims=True))
        offset = offset + jnp.sum(jnp.where(hot, 1.0, 0.0), axis=1, keepdims=True)
    rank = jnp.concatenate(ranks, axis=1)
    place = dest * SLOTS + rank.astype(jnp.int32)
    high = (cell >> 5) + 1
    low = cell & 31
    row = iota((16, COUNT), 0)
    meta = jnp.where(row == 0, high, jnp.where(row == 1, low, 0)).astype(F32).astype(BF)
    traces = traces_ref[...]
    blank = jnp.zeros((EXTRA, TS - SLOTS), F32)
    step = 8
    copies = []
    for o in range(0, OWNERS, step):
        slot = iota((step * SLOTS, COUNT), 0) + o * SLOTS
        placing = onehot(slot == place)
        rows = dot(placing, traces).astype(BF)
        extra = dot_t(meta, placing)
        for k in range(step):
            out_ref[o + k, 0:SLOTS, :] = rows[k * SLOTS : (k + 1) * SLOTS]
            part = extra[0:EXTRA, k * SLOTS : (k + 1) * SLOTS]
            out_ref[o + k, SLOTS:PAY, :] = jnp.concatenate([part, blank], axis=1).astype(BF)
        copy = pltpu.make_async_copy(out_ref.at[o : o + step], out_hbm.at[o : o + step], sems.at[o // step])
        copy.start()
        copies.append(copy)
    token_ref[...] = jnp.zeros(token_ref.shape, F32) + rank[:, 0:128]
    for copy in copies:
        copy.wait()


def weights_kernel(first_ref, mid_ref, last_ref, bias_ref, token_ref, w1_ref, w2_ref, w3_ref, w4_ref):
    bias = 0.5 * bias_ref[...]
    parts = []
    for _ in range(3):
        part = bias.astype(BF)
        parts.append(part)
        bias = bias - part.astype(F32)

    def bias_columns(spread, layer):
        row = iota((16, CH), 0)
        lines = jnp.zeros((16, CH), F32)
        for e in range(3):
            lines = jnp.where(row == e, parts[e][layer : layer + 1].astype(F32), lines)
        spreaded = dot_t(spread, lines.astype(BF)).astype(BF)
        return dot(spreaded, onehot(iota((16, KDIM), 1) == iota((16, KDIM), 0) + TAPS))

    step = 6 * CH
    first = first_ref[...]
    c = iota((step, KDIM), 1)
    b = jnp.where(c >= 80, 1, 0) + jnp.where(c >= 160, 1, 0)
    m = jnp.where(c < TAPS, c - 80 * b, -100)
    ck = iota((9, KDIM), 1)
    bk = jnp.where(ck >= 80, 1, 0) + jnp.where(ck >= 160, 1, 0)
    spread = onehot((iota((step, CH), 0) & (CH - 1)) == iota((step, CH), 1))
    base = dot(spread, first).astype(BF)
    picked = [0.5 * dot(base, onehot(iota((9, KDIM), 0) == 3 * a + bk)) for a in range(3)]
    other = bias_columns(spread, 0)
    for n in range(R1 * CH // step):
        r = (iota((step, KDIM), 0) >> 4) + 6 * n
        r = jnp.where(r < R1 // 2, 2 * r, 2 * r - (R1 - 1))
        total = other
        for a in range(3):
            total = jnp.where(m - r == a, picked[a], total)
        w1_ref[n * step : (n + 1) * step, :] = total.astype(BF)
    rows = GROUP * CH
    spread = onehot((iota((rows, CH), 0) & (CH - 1)) == iota((rows, CH), 1))
    c = iota((rows, KDIM), 1)
    b = jnp.where(c >= 80, 1, 0) + jnp.where(c >= 160, 1, 0)
    delta = jnp.where(c < TAPS, ((c - 80 * b) >> 4) - (iota((rows, KDIM), 0) >> 4), -100)
    ck = iota((144, KDIM), 1)
    bk = jnp.where(ck >= 80, 1, 0) + jnp.where(ck >= 160, 1, 0)
    for layer, out_ref in ((0, w2_ref), (1, w3_ref)):
        base = dot(spread, mid_ref[layer]).astype(BF)
        total = bias_columns(spread, layer + 1)
        for a in range(3):
            pick = onehot(iota((144, KDIM), 0) == (3 * a + bk) * CH + (ck & 15))
            total = jnp.where(delta == a, 0.5 * dot(base, pick), total)
        out_ref[...] = total.astype(BF)
    last = jnp.broadcast_to(last_ref[...], (24, 144))
    delta = (iota((24, 160), 1) >> 4) - (iota((24, 160), 0) & 7)
    tap = iota((24, 160), 0) >> 3
    col = iota((144, 160), 1) & 15
    total = jnp.zeros((24, 160), F32)
    for b in range(3):
        for a in range(3):
            line = dot(last, onehot(iota((144, 160), 0) == (3 * a + b) * CH + col))
            total = jnp.where((delta == a) & (tap == b), line, total)
    w4_ref[...] = total.astype(BF)


def stack_kernel(recv_ref, w1_ref, pos_ref, out_ref, left_ref, right_ref):
    cells = []
    for s in range(OWNERS):
        extra = recv_ref[s, SLOTS:PAY, 0:SLOTS].astype(F32)
        cells.append((extra[0:1] - 1.0) * 32.0 + extra[1:2])
    cell = jnp.concatenate(cells, axis=1).astype(jnp.int32)
    total = OWNERS * SLOTS
    rows = recv_ref[:, 0:SLOTS, :].reshape(total, TS)
    lefts, rights = [], []
    step = 4
    for c in range(0, CL, step):
        hit = jnp.where(iota((step * MB, total), 0) + c * MB == cell, 1.0, 0.0)
        fold = jnp.maximum(jnp.sum(hit, axis=1, keepdims=True), 1.0)
        part = dot(hit.astype(BF), rows) / fold
        for k in range(step):
            piece = part[k * MB : (k + 1) * MB]
            out_ref[c + k] = piece.astype(BF)
            lefts.append(piece[:, 0:HALO])
            rights.append(piece[:, TS - HALO :])
    left_ref[...] = jnp.concatenate(lefts, axis=1).astype(BF)
    right_ref[...] = jnp.concatenate(rights, axis=1).astype(BF)


def transposed(blocks):
    group = iota(blocks[0].shape, 1) >> 4
    blocks = list(blocks)
    for bit in (1, 2, 4):
        keep = (group & bit) == 0
        for i in range(8):
            if i & bit == 0:
                a, b = blocks[i], blocks[i | bit]
                blocks[i] = jnp.where(keep, a, pltpu.roll(b, 16 * bit, 1))
                blocks[i | bit] = jnp.where(keep, pltpu.roll(a, TILE - 16 * bit, 1), b)
    return blocks


def swap_kernel(stack_ref, low_ref, high_ref, out_ref, first_ref, last_ref):
    side = jnp.concatenate([low_ref[...].astype(F32), high_ref[...].astype(F32)], axis=1)
    owner = (iota((MB, TILE), 1) >> 3) & 7
    rows = TS + TILE
    row = iota((rows, 1), 0)
    tau = row + HALO
    tau = jnp.where(row >= TS, row & 7, tau)
    tau = jnp.where(row >= TS + TILE // 2, (row & 7) + TS + HALO, tau)
    col = iota((1, 3 * TILE), 1)
    order = onehot(tau == TILES * (col & 15) + jnp.minimum(col >> 4, TILES - 1))
    full = []
    for c in range(CL):
        full.append(jnp.concatenate([stack_ref[c], jnp.where(owner == c, side, 0.0).astype(BF)], axis=1))
    mixed = dot(jnp.concatenate(full, axis=0), order)
    for half in range(2):
        blocks = [mixed[c * MB : (c + 1) * MB, half * TILE : (half + 1) * TILE] for c in range(CL)]
        for k, tile in enumerate(transposed(blocks)):
            k = 8 * half + k
            out_ref[:, k * TILE : (k + 1) * TILE] = tile.astype(BF)
    lane = iota((MB, TILE), 1) >> 4
    tile = jnp.zeros((MB, TILE), F32)
    for c in range(CL):
        tile = jnp.where(lane == c, mixed[c * MB : (c + 1) * MB, 2 * TILE :], tile)
    out_ref[:, 16 * TILE :] = tile.astype(BF)
    first_ref[...] = out_ref[0:HALO, :]
    last_ref[...] = out_ref[MB - HALO : MB, :]


def gelu_half(h):
    c0 = 2.0 * 0.7978845608028654
    c1 = 8.0 * 0.7978845608028654 * 0.044715
    return h + h * jnp.tanh(h * (c0 + c1 * (h * h)))


def turned(block, shift):
    return pltpu.roll(block, shift % TILE, 1)


def conv_kernel(pos_ref, core_ref, low_ref, high_ref, stack_ref, w1_ref, w2_ref, w3_ref, w4_ref, out_ref,
                x_ref, h1_ref, h2_ref, h3_ref, p_ref, mask_ref):
    mid = pos_ref[0]
    tm = pos_ref[1]
    lane = iota((CH, WIDE), 1)
    t = TILES * ((lane & 127) & 15) + (lane >> 7) - HALO + tm * TS
    keep = jnp.where((t >= 0) & (t < 4 * TS), 1.0, 0.0)
    mask_ref[0] = keep.astype(BF)
    mask_ref[1] = (keep * jnp.where(mid > 0, 1.0, 0.0)).astype(BF)
    mask_ref[2] = (keep * jnp.where(mid < 7, 1.0, 0.0)).astype(BF)

    def at(k):
        return slice((LEAD + k) * TILE, (LEAD + k + 1) * TILE)

    image = jnp.concatenate([low_ref[...].astype(F32), core_ref[...].astype(F32), high_ref[...].astype(F32)], axis=0)
    x_ref[:, TILE : TILE + LANES] = image.astype(BF)
    x_ref[:, 0:TILE] = pltpu.roll(image[:, 16 * TILE :], 1, 1).astype(BF)
    for k in range(2):
        x_ref[:, (18 + k) * TILE : (19 + k) * TILE] = pltpu.roll(image[:, k * TILE : (k + 1) * TILE], TILE - 1, 1).astype(BF)
    ones = jnp.ones((KDIM - TAPS, CHUNK), BF)
    chunks = [(k * CHUNK, min(CHUNK, LANES - k * CHUNK)) for k in range(NCHUNK)]
    h1_ref[R1 * CH :, :] = jnp.zeros((2 * CH, EXT), BF)
    h1_ref[:, (LEAD + 19) * TILE :] = jnp.zeros((80 * CH, 3 * TILE), BF)
    h2_ref[:, (LEAD + 21) * TILE :] = jnp.zeros((R2 * CH, TILE), BF)

    def finish(acc, row, base, wide, into_ref, slot, lead):
        which = 1 if row < 0 else (2 if row >= MB else 0)
        g = gelu_half(acc).astype(BF) * mask_ref[which, :, base : base + wide]
        into_ref[slot * CH : (slot + 1) * CH, base + lead * TILE : base + lead * TILE + wide] = g

    def layer1(base, wide):
        x = [x_ref[:, base + b * TILE : base + b * TILE + wide] for b in range(3)]
        x = jnp.concatenate(x + [ones[:, :wide]], axis=0)
        for s0 in range(0, R1, 13):
            acc = dot(w1_ref[s0 * CH : (s0 + 13) * CH, :], x)
            for j in range(13):
                finish(acc[j * CH : (j + 1) * CH], ORDER1[s0 + j] - 7, base, wide, h1_ref, s0 + j, LEAD)

    def window(ref, s0, base, wide, d):
        taps = []
        for b in range(3):
            lane = base + (LEAD + (b - 1) * d) * TILE
            taps.append(ref[s0 * CH : (s0 + 5) * CH, lane : lane + wide])
        return jnp.concatenate(taps + [ones[:, :wide]], axis=0)

    def layer2(base, wide):
        for s0 in range(0, R1 - 2, GROUP):
            acc = dot(w2_ref[...], window(h1_ref, s0, base, wide, 2))
            for j in range(GROUP):
                if s0 + j < R1 and ORDER1[s0 + j] < R2:
                    q = ORDER1[s0 + j]
                    finish(acc[j * CH : (j + 1) * CH], q - 5, base, wide, h2_ref, SLOT2[q], LEAD)

    def layer3(base, wide):
        for s0 in range(0, R2 - 2, GROUP):
            acc = dot(w3_ref[...], window(h2_ref, s0, base, wide, 4))
            for j in range(GROUP):
                if ORDER2[s0 + j] < R3:
                    q = ORDER2[s0 + j]
                    finish(acc[j * CH : (j + 1) * CH], q - 1, base, wide, h3_ref, q, 0)

    def layer4(base, wide):
        for q in range(0, MB, 8):
            acc = dot(w4_ref[...], h3_ref[q * CH : (q + 10) * CH, base : base + wide])
            for b in range(3):
                p_ref[b, q : q + 8, base + TILE : base + TILE + wide] = acc[8 * b : 8 * b + 8]

    def carry(ref, rows, width):
        for k in range(width):
            ref[:rows, at(TILES + k)] = turned(ref[:rows, at(k)], -1)
            ref[:rows, at(-1 - k)] = turned(ref[:rows, at(TILES - 1 - k)], 1)

    for n in range(NCHUNK):
        layer1(*chunks[n])
    carry(h1_ref, R1 * CH, 2)
    for n in (1, 2, 3, 4, 5, 6, 7, 8, 0):
        layer2(*chunks[n])
    carry(h2_ref, R2 * CH, 4)
    for n in (3, 4, 5, 6, 7, 8, 0, 1, 2):
        layer3(*chunks[n])
        layer4(*chunks[n])
    p_ref[0, :, 0:TILE] = pltpu.roll(p_ref[0, :, TILES * TILE : (TILES + 1) * TILE], 1, 1)
    p_ref[2, :, (TILES + 1) * TILE : (TILES + 2) * TILE] = pltpu.roll(p_ref[2, :, TILE : 2 * TILE], TILE - 1, 1)
    tiles = [
        p_ref[0, :, k * TILE : (k + 1) * TILE]
        + p_ref[1, :, (k + 1) * TILE : (k + 2) * TILE]
        + p_ref[2, :, (k + 2) * TILE : (k + 3) * TILE]
        for k in range(TILES)
    ]
    col = iota((3 * TILE, 1), 0)
    tau = jnp.where(col < SEG, TILES * (col & 15) + (col >> 4), -1)
    order = onehot(tau == iota((1, TS), 1) + HALO)
    firsts, seconds = transposed(tiles[0:8]), transposed(tiles[8:16])
    for c in range(CL):
        third = pltpu.roll(tiles[16], TILE - 16 * c, 1) if c else tiles[16]
        noise = jnp.concatenate([firsts[c], seconds[c], third], axis=1)
        top = noise.astype(BF)
        rest = (noise - top.astype(F32)).astype(BF)
        both = dot(jnp.concatenate([top, rest], axis=0), order)
        out_ref[c] = stack_ref[c].astype(F32) - (both[0:MB] + both[MB:])


def call(kernel, outs, scratch=(), smem=0, n=0, loose=0, name=None, limit=20, where=None):
    specs = [pl.BlockSpec(memory_space=pltpu.SMEM) for _ in range(smem)]
    specs += [pl.BlockSpec(memory_space=pltpu.VMEM) for _ in range(n)]
    specs += [pl.BlockSpec(memory_space=pl.ANY) for _ in range(loose)]
    number = len(outs) if isinstance(outs, tuple) else 1
    out_specs = tuple(pl.BlockSpec(memory_space=space) for space in where or (pltpu.VMEM,) * number)
    return pl.pallas_call(
        kernel,
        out_shape=outs,
        in_specs=specs,
        out_specs=out_specs if isinstance(outs, tuple) else out_specs[0],
        scratch_shapes=list(scratch),
        compiler_params=pltpu.CompilerParams(vmem_limit_bytes=limit * 2**20),
        name=name,
    )


def shape(*dims, dtype=BF):
    return pltpu.VMEM(dims, dtype)


def near(x):
    return pltpu.with_memory_space_constraint(x, pltpu.VMEM)


def build_send(dest, cell, traces):
    outs = (jax.ShapeDtypeStruct((OWNERS, PAY, TS), BF), jax.ShapeDtypeStruct((8, 128), F32))
    scratch = [pltpu.VMEM((OWNERS, PAY, TS), BF), pltpu.SemaphoreType.DMA((4,))]
    return call(send_kernel, outs, scratch, n=3, name="send", where=(pl.ANY, pltpu.VMEM))(dest, cell, traces)


def build_weights(w_first, w_mid, w_last, bias, token):
    outs = (shape(R1 * CH, KDIM), shape(GROUP * CH, KDIM), shape(GROUP * CH, KDIM), shape(24, 160))
    return call(weights_kernel, outs, n=5, name="weights")(w_first, w_mid, w_last, bias, token)


def build_stack(recv, w1, pos):
    outs = (shape(CL, MB, TS), shape(MB, MB), shape(MB, MB))
    return call(stack_kernel, outs, n=1, loose=2, name="stack")(near(recv), w1, pos)


def reorder(stack, low, high):
    outs = (shape(MB, LANES), shape(HALO, LANES), shape(HALO, LANES))
    return call(swap_kernel, outs, n=3, name="reorder")(near(stack), near(low), near(high))


def convolve(pos, core, low, high, stack, weights):
    scratch = [
        pltpu.VMEM((80, 20 * TILE), BF),
        pltpu.VMEM((80 * CH, EXT), BF),
        pltpu.VMEM((R2 * CH, EXT), BF),
        pltpu.VMEM((R3 * CH, WIDE), BF),
        pltpu.VMEM((3, MB, 20 * TILE), F32),
        pltpu.VMEM((3, CH, WIDE), BF),
    ]
    return call(conv_kernel, jax.ShapeDtypeStruct((CL, MB, TS), F32), scratch, smem=1, n=8, name="conv", limit=40)(
        pos, near(core), near(low), near(high), near(stack), *[near(w) for w in weights]
    )


def neighbours(low_edge, high_edge, axis):
    count = lax.axis_size(axis)
    up = [(i, i + 1) for i in range(count - 1)]
    down = [(b, a) for a, b in up]
    return lax.ppermute(high_edge, axis, up), lax.ppermute(low_edge, axis, down)


def shards(traces, dest, cell, w_first, w_mid, w_last, bias):
    send, token = build_send(dest.reshape(1, COUNT), cell.reshape(1, COUNT), traces)
    recv = lax.all_to_all(send, ("offset", "mid"), split_axis=0, concat_axis=0, tiled=True)
    weights = build_weights(w_first, w_mid, w_last, bias, token)
    pos = jnp.stack([lax.axis_index("mid"), lax.axis_index("tm")]).astype(jnp.int32)
    stack, left, right = build_stack(recv, weights[0], pos)
    low, high = neighbours(left, right, "tm")
    core, first, last = reorder(stack, low, high)
    below, above = neighbours(first, last, "mid")
    return convolve(pos, core, below, above, stack, weights)


def solution(mesh):
    rows = P(("offset", "mid"), "tm")
    column = P(("offset", "mid"), None)
    placed = (rows, column, column, P(), P(), P(), P())
    return jax.shard_map(
        shards, mesh=mesh, in_specs=placed, out_specs=P("offset", "mid", "tm"), check_vma=False
    )
```

profile of v0, /device:TPU:1, one launch (start us, length us, event | category | flops | bytes accessed | tf_op | source)
XLA Modules:
  0.0 66.8 jit_solution(16913501309499303592)
XLA Ops:
  0.0 1.0 %copy-done = bf16[1024,256]{1,0:T(8,128)(2,1)S(1)} copy-done((bf16[1024,256]{1,0:T(8,128)(2,1)S(1)}, bf16[1024,256]{1,0:T(8,128)(2,1)}, u32[]{:S(2)}) %copy-start) | copy-done | bytes 524312
  1.0 0.7 %copy-done.2 = s32[1024,1]{0,1:T(1,128)S(1)} copy-done((s32[1024,1]{0,1:T(1,128)S(1)}, s32[1024,1]{0,1:T(1,128)}, u32[]{:S(2)}) %copy-start.2) | copy-done | bytes 4120
  1.7 0.7 %copy-done.3 = s32[1024,1]{0,1:T(1,128)S(1)} copy-done((s32[1024,1]{0,1:T(1,128)S(1)}, s32[1024,1]{0,1:T(1,128)}, u32[]{:S(2)}) %copy-start.3) | copy-done | bytes 4120
  2.4 3.3 %send.1 = (bf16[32,72,256]{2,1,0:T(8,128)(2,1)}, f32[8,128]{1,0:T(8,128)S(1)}) custom-call(s32[1,1024]{1,0:T(1,128)S(1)} %bitcast.4, s32[1,1024]{1,0:T(1,128)S(1)} %bitcast.5, bf16[1024,256]{1,0:T(8,128)(2,1)S(1)} %copy-done), custom_call_target="tpu_custom_call" | custom-call | tf_op jit(solution)/shard_map/send/pallas_call | solution.py:368
  5.8 0.0 copy-start.1
  5.8 0.0 copy-start.4
  5.8 0.0 copy-start.5
  5.8 0.0 copy-start.6
  5.8 9.6 %all-to-all-start = ((bf16[32,72,256]{2,1,0:T(8,128)(2,1)}), bf16[32,72,256]{2,1,0:T(8,128)(2,1)S(1)}, u32[]{:S(2)}, u32[]{:S(2)}) async-start(bf16[32,72,256]{2,1,0:T(8,128)(2,1)} %get-tuple-element.17), calls=%async_computation | async-start | bytes 2359296 | tf_op jit(solution)/shard_map/all_to_all | solution.py:409
  15.4 0.0 copy-done.1
  15.4 1.1 %weights.1 = (bf16[1248,256]{1,0:T(8,128)(2,1)S(1)}, bf16[48,256]{1,0:T(8,128)(2,1)S(1)}, bf16[48,256]{1,0:T(8,128)(2,1)S(1)}, bf16[24,160]{1,0:T(8,128)(2,1)S(1)}) custom-call(bf16[16,9]{1,0:T(8,128)(2,1)S(1)} %copy-done.4, bf16[2,16,144]{2,1,0:T(8,128)(2,1)S(1)} %copy-done.1, bf16[1,144]{1,0:T(2,128)(2,1)S(1)} %copy-done.6, f32[3,16]{1,0:T(4,128)S(1)} %copy-done.5, ...), custom_call_target="tpu_custom_call" | custom-call | tf_op jit(solution)/shard_map/weights/pallas_call | solution.py:373
  16.6 0.1 pad_add_fusion.pos_ref
  16.6 17.1 %all-to-all-done.recv_ref = bf16[32,72,256]{2,1,0:T(8,128)(2,1)S(1)} async-done(((bf16[32,72,256]{2,1,0:T(8,128)(2,1)}), bf16[32,72,256]{2,1,0:T(8,128)(2,1)S(1)}, u32[]{:S(2)}, u32[]{:S(2)}) %all-to-all-start) | async-done | bytes 1179680 | tf_op jit(solution)/shard_map/all_to_all | solution.py:409
  33.7 1.3 %stack.13 = (bf16[8,64,256]{2,1,0:T(8,128)(2,1)S(1)}, bf16[64,64]{1,0:T(8,128)(2,1)S(1)}, bf16[64,64]{1,0:T(8,128)(2,1)S(1)}) custom-call(bf16[32,72,256]{2,1,0:T(8,128)(2,1)S(1)} %all-to-all-done.recv_ref, bf16[1248,256]{1,0:T(8,128)(2,1)S(1)} %get-tuple-element.19.w1_ref, s32[2]{0:T(128)S(1)} %pad_add_fusion.pos_ref), custom_call_target="tpu_custom_call" | custom-call | tf_op jit(solution)/shard_map/stack/pallas_call | solution.py:378
  35.0 3.2 %collective-permute-start = (bf16[64,64]{1,0:T(8,128)(2,1)S(1)}, bf16[64,64]{1,0:T(8,128)(2,1)S(1)}, u32[]{:S(2)}, u32[]{:S(2)}) collective-permute-start(bf16[64,64]{1,0:T(8,128)(2,1)S(1)} %get-tuple-element.21), channel_id=1, source_target_pairs={{0,1},{1,2},{2,3},{4,5},{5,6},{6,7},{8,9},{9,10},{10,11},{12,13},{... | collective-permute-start | bytes 24584 | tf_op jit(solution)/shard_map/ppermute | solution.py:404
  38.2 1.3 %collective-permute-start.1 = (bf16[64,64]{1,0:T(8,128)(2,1)S(1)}, bf16[64,64]{1,0:T(8,128)(2,1)S(1)}, u32[]{:S(2)}, u32[]{:S(2)}) collective-permute-start(bf16[64,64]{1,0:T(8,128)(2,1)S(1)} %get-tuple-element.22), channel_id=1, source_target_pairs={{1,0},{2,1},{3,2},{5,4},{6,5},{7,6},{9,8},{10,9},{11,10},{13,12},{... | collective-permute-start | bytes 24584 | tf_op jit(solution)/shard_map/ppermute | solution.py:404
  39.5 0.0 collective-permute-done.low_ref
  39.6 3.2 %collective-permute-done.1.high_ref = bf16[64,64]{1,0:T(8,128)(2,1)S(1)} collective-permute-done((bf16[64,64]{1,0:T(8,128)(2,1)S(1)}, bf16[64,64]{1,0:T(8,128)(2,1)S(1)}, u32[]{:S(2)}, u32[]{:S(2)}) %collective-permute-start.1) | collective-permute-done | bytes 8224 | tf_op jit(solution)/shard_map/ppermute | solution.py:404
  42.7 0.6 reorder.1
  43.4 3.4 %collective-permute-start.2 = (bf16[8,2176]{1,0:T(8,128)(2,1)S(1)}, bf16[8,2176]{1,0:T(8,128)(2,1)S(1)}, u32[]{:S(2)}, u32[]{:S(2)}) collective-permute-start(bf16[8,2176]{1,0:T(8,128)(2,1)S(1)} %get-tuple-element.24), channel_id=1, source_target_pairs={{0,4},{4,8},{8,12},{12,16},{16,20},{20,24},{24,28},{1,5},{5,9},{9,... | collective-permute-start | bytes 104456 | tf_op jit(solution)/shard_map/ppermute | solution.py:404
  46.8 2.1 %collective-permute-start.3 = (bf16[8,2176]{1,0:T(8,128)(2,1)S(1)}, bf16[8,2176]{1,0:T(8,128)(2,1)S(1)}, u32[]{:S(2)}, u32[]{:S(2)}) collective-permute-start(bf16[8,2176]{1,0:T(8,128)(2,1)S(1)} %get-tuple-element.25), channel_id=1, source_target_pairs={{4,0},{8,4},{12,8},{16,12},{20,16},{24,20},{28,24},{5,1},{9,5},{13... | collective-permute-start | bytes 104456 | tf_op jit(solution)/shard_map/ppermute | solution.py:404
  48.9 0.0 collective-permute-done.2.low_ref
  48.9 3.1 %collective-permute-done.3.high_ref = bf16[8,2176]{1,0:T(8,128)(2,1)S(1)} collective-permute-done((bf16[8,2176]{1,0:T(8,128)(2,1)S(1)}, bf16[8,2176]{1,0:T(8,128)(2,1)S(1)}, u32[]{:S(2)}, u32[]{:S(2)}) %collective-permute-start.3) | collective-permute-done | bytes 34848 | tf_op jit(solution)/shard_map/ppermute | solution.py:404
  52.1 14.8 %conv.1 = f32[8,64,256]{2,1,0:T(8,128)} custom-call(s32[2]{0:T(128)S(1)} %pad_add_fusion.pos_ref, bf16[64,2176]{1,0:T(8,128)(2,1)S(1)} %get-tuple-element.23.core_ref, bf16[8,2176]{1,0:T(8,128)(2,1)S(1)} %collective-permute-done.2.low_ref, bf16[8,2176]{1,0:T(8,128)(2,1)S(1)} %collective-permute-done.3.high_ref, ...), custom_call_target="tpu_custom_call" | custom-call | tf_op jit(solution)/shard_map/conv/pallas_call | solution.py:395
  (6 shorter events, 0.0 us)
Async XLA Ops:
  0.0 1.0 %copy-start = (bf16[1024,256]{1,0:T(8,128)(2,1)S(1)}, bf16[1024,256]{1,0:T(8,128)(2,1)}, u32[]{:S(2)}) copy-start(bf16[1024,256]{1,0:T(8,128)(2,1)} %traces_ref.1) | copy-start | bytes 1572868
  1.0 0.7 %copy-start.2 = (s32[1024,1]{0,1:T(1,128)S(1)}, s32[1024,1]{0,1:T(1,128)}, u32[]{:S(2)}) copy-start(s32[1024,1]{0,1:T(1,128)} %param.8) | copy-start | bytes 12292
  1.7 0.7 %copy-start.3 = (s32[1024,1]{0,1:T(1,128)S(1)}, s32[1024,1]{0,1:T(1,128)}, u32[]{:S(2)}) copy-start(s32[1024,1]{0,1:T(1,128)} %param.9) | copy-start | bytes 12292
  5.8 9.6 %copy-start.1 = (bf16[2,16,144]{2,1,0:T(8,128)(2,1)S(1)}, bf16[2,16,144]{2,1,0:T(8,128)(2,1)}, u32[]{:S(2)}) copy-start(bf16[2,16,144]{2,1,0:T(8,128)(2,1)} %mid_ref.1) | copy-start | bytes 27652
  5.8 9.6 %copy-start.4 = (bf16[16,9]{1,0:T(8,128)(2,1)S(1)}, bf16[16,9]{1,0:T(8,128)(2,1)}, u32[]{:S(2)}) copy-start(bf16[16,9]{1,0:T(8,128)(2,1)} %first_ref.1) | copy-start | bytes 868
  5.8 9.6 %copy-start.5 = (f32[3,16]{1,0:T(4,128)S(1)}, f32[3,16]{1,0:T(4,128)}, u32[]{:S(2)}) copy-start(f32[3,16]{1,0:T(4,128)} %bias_ref.1) | copy-start | bytes 580
  5.8 9.6 %copy-start.6 = (bf16[1,144]{1,0:T(2,128)(2,1)S(1)}, bf16[1,144]{1,0:T(2,128)(2,1)}, u32[]{:S(2)}) copy-start(bf16[1,144]{1,0:T(2,128)(2,1)} %last_ref.1) | copy-start | bytes 868
  5.8 27.9 %all-to-all-start = ((bf16[32,72,256]{2,1,0:T(8,128)(2,1)}), bf16[32,72,256]{2,1,0:T(8,128)(2,1)S(1)}, u32[]{:S(2)}, u32[]{:S(2)}) async-start(bf16[32,72,256]{2,1,0:T(8,128)(2,1)} %get-tuple-element.17), calls=%async_computation | async-start | bytes 2359296 | tf_op jit(solution)/shard_map/all_to_all | solution.py:409
  35.0 4.5 %collective-permute-start = (bf16[64,64]{1,0:T(8,128)(2,1)S(1)}, bf16[64,64]{1,0:T(8,128)(2,1)S(1)}, u32[]{:S(2)}, u32[]{:S(2)}) collective-permute-start(bf16[64,64]{1,0:T(8,128)(2,1)S(1)} %get-tuple-element.21), channel_id=1, source_target_pairs={{0,1},{1,2},{2,3},{4,5},{5,6},{6,7},{8,9},{9,10},{10,11},{12,13},{... | collective-permute-start | bytes 24584 | tf_op jit(solution)/shard_map/ppermute | solution.py:404
  38.2 4.5 %collective-permute-start.1 = (bf16[64,64]{1,0:T(8,128)(2,1)S(1)}, bf16[64,64]{1,0:T(8,128)(2,1)S(1)}, u32[]{:S(2)}, u32[]{:S(2)}) collective-permute-start(bf16[64,64]{1,0:T(8,128)(2,1)S(1)} %get-tuple-element.22), channel_id=1, source_target_pairs={{1,0},{2,1},{3,2},{5,4},{6,5},{7,6},{9,8},{10,9},{11,10},{13,12},{... | collective-permute-start | bytes 24584 | tf_op jit(solution)/shard_map/ppermute | solution.py:404
  43.4 5.6 %collective-permute-start.2 = (bf16[8,2176]{1,0:T(8,128)(2,1)S(1)}, bf16[8,2176]{1,0:T(8,128)(2,1)S(1)}, u32[]{:S(2)}, u32[]{:S(2)}) collective-permute-start(bf16[8,2176]{1,0:T(8,128)(2,1)S(1)} %get-tuple-element.24), channel_id=1, source_target_pairs={{0,4},{4,8},{8,12},{12,16},{16,20},{20,24},{24,28},{1,5},{5,9},{9,... | collective-permute-start | bytes 104456 | tf_op jit(solution)/shard_map/ppermute | solution.py:404
  46.8 5.3 %collective-permute-start.3 = (bf16[8,2176]{1,0:T(8,128)(2,1)S(1)}, bf16[8,2176]{1,0:T(8,128)(2,1)S(1)}, u32[]{:S(2)}, u32[]{:S(2)}) collective-permute-start(bf16[8,2176]{1,0:T(8,128)(2,1)S(1)} %get-tuple-element.25), channel_id=1, source_target_pairs={{4,0},{8,4},{12,8},{16,12},{20,16},{24,20},{28,24},{5,1},{9,5},{13... | collective-permute-start | bytes 104456 | tf_op jit(solution)/shard_map/ppermute | solution.py:404
where the time goes:
time: 67.3 us; the launch traced here: 66.8 us
  waiting for transfers between devices  23.4 us (35%)
  Pallas kernels  21.2 us (32%)
  starting transfers between devices  19.6 us (29%)
  local copies, waits for them, and re-layouts  2.44 us (4%)
    all_to_all x1, waiting for transfers between devices, shards(): lax.all_to_all(send, ('offset', 'mid'), split_axis=0, concat_axis=0, tile...  17.1 us
    pallas_call x1, Pallas kernels, convolve(): call(conv_kernel, jax.ShapeDtypeStruct((CL, MB, TS), F32), scratch, smem=...  14.8 us
    all_to_all x1, starting transfers between devices, shards(): lax.all_to_all(send, ('offset', 'mid'), split_axis=0, concat_axis=0, tile...  9.56 us
    ppermute x2, starting transfers between devices, neighbours(): lax.ppermute(high_edge, axis, up)  6.63 us
    ppermute x2, waiting for transfers between devices, neighbours(): lax.ppermute(low_edge, axis, down)  6.31 us
    ppermute x2, starting transfers between devices, neighbours(): lax.ppermute(low_edge, axis, down)  3.39 us
    pallas_call x1, Pallas kernels, build_send(): call(send_kernel, outs, scratch, n=3, name='send', where=(pl.ANY, pltpu.V...  3.33 us
    unnamed x14, local copies, waits for them, and re-layouts  2.44 us
  transfers between devices with their start and end apart: 5, of which 3 were waited for; matrix products, arithmetic and copies ran while one was open for 0% of the time, Pallas kernels for 2%

commit v1 on v0

--- a/solution.py
+++ b/solution.py
@@ -31,7 +31,7 @@
 KDIM = 256
 GROUP = 3
 EXTRA = 8
-PAY = SLOTS + EXTRA
+PAY = 2 * SLOTS + EXTRA
 
 
 def slots_of(rows, groups):
@@ -59,7 +59,15 @@
     return lax.dot_general(a, b, (((1,), (1,)), ((), ())), preferred_element_type=F32)
 
 
-def send_kernel(dest_ref, cell_ref, traces_ref, out_hbm, token_ref, out_ref, sems):
+def send_kernel(dest_hbm, cell_hbm, traces_hbm, out_hbm, token_ref, out_ref, sems, dest_ref, cell_ref, traces_ref, ins):
+    loads = [
+        pltpu.make_async_copy(source, target, ins.at[n])
+        for n, (source, target) in enumerate(((dest_hbm, dest_ref), (cell_hbm, cell_ref), (traces_hbm, traces_ref)))
+    ]
+    for load in loads:
+        load.start()
+    for load in loads[:2]:
+        load.wait()
     dest = dest_ref[...]
     cell = cell_ref[...]
     width = 256
@@ -80,8 +88,9 @@
     low = cell & 31
     row = iota((16, COUNT), 0)
     meta = jnp.where(row == 0, high, jnp.where(row == 1, low, 0)).astype(F32).astype(BF)
+    loads[2].wait()
     traces = traces_ref[...]
-    blank = jnp.zeros((EXTRA, TS - SLOTS), F32)
+    blank = jnp.zeros((EXTRA, TILE - SLOTS), F32)
     step = 8
     copies = []
     for o in range(0, OWNERS, step):
@@ -90,9 +99,10 @@
         rows = dot(placing, traces).astype(BF)
         extra = dot_t(meta, placing)
         for k in range(step):
-            out_ref[o + k, 0:SLOTS, :] = rows[k * SLOTS : (k + 1) * SLOTS]
+            out_ref[o + k, 0:SLOTS, :] = rows[k * SLOTS : (k + 1) * SLOTS, 0:TILE]
+            out_ref[o + k, SLOTS : 2 * SLOTS, :] = rows[k * SLOTS : (k + 1) * SLOTS, TILE:]
             part = extra[0:EXTRA, k * SLOTS : (k + 1) * SLOTS]
-            out_ref[o + k, SLOTS:PAY, :] = jnp.concatenate([part, blank], axis=1).astype(BF)
+            out_ref[o + k, 2 * SLOTS : PAY, :] = jnp.concatenate([part, blank], axis=1).astype(BF)
         copy = pltpu.make_async_copy(out_ref.at[o : o + step], out_hbm.at[o : o + step], sems.at[o // step])
         copy.start()
         copies.append(copy)
@@ -164,11 +174,13 @@
 def stack_kernel(recv_ref, w1_ref, pos_ref, out_ref, left_ref, right_ref):
     cells = []
     for s in range(OWNERS):
-        extra = recv_ref[s, SLOTS:PAY, 0:SLOTS].astype(F32)
+        extra = recv_ref[s, 2 * SLOTS : PAY, 0:SLOTS].astype(F32)
         cells.append((extra[0:1] - 1.0) * 32.0 + extra[1:2])
     cell = jnp.concatenate(cells, axis=1).astype(jnp.int32)
     total = OWNERS * SLOTS
-    rows = recv_ref[:, 0:SLOTS, :].reshape(total, TS)
+    rows = jnp.concatenate(
+        [recv_ref[:, 0:SLOTS, :].reshape(total, TILE), recv_ref[:, SLOTS : 2 * SLOTS, :].reshape(total, TILE)], axis=1
+    )
     lefts, rights = [], []
     step = 4
     for c in range(0, CL, step):
@@ -235,8 +247,8 @@
     return pltpu.roll(block, shift % TILE, 1)
 
 
-def conv_kernel(pos_ref, core_ref, low_ref, high_ref, stack_ref, w1_ref, w2_ref, w3_ref, w4_ref, out_ref,
-                x_ref, h1_ref, h2_ref, h3_ref, p_ref, mask_ref):
+def conv_kernel(pos_ref, core_ref, low_ref, high_ref, stack_ref, w1_ref, w2_ref, w3_ref, w4_ref, out_hbm,
+                out_ref, sems, x_ref, h1_ref, h2_ref, h3_ref, p_ref, mask_ref):
     mid = pos_ref[0]
     tm = pos_ref[1]
     lane = iota((CH, WIDE), 1)
@@ -327,6 +339,7 @@
     col = iota((3 * TILE, 1), 0)
     tau = jnp.where(col < SEG, TILES * (col & 15) + (col >> 4), -1)
     order = onehot(tau == iota((1, TS), 1) + HALO)
+    copies = []
     firsts, seconds = transposed(tiles[0:8]), transposed(tiles[8:16])
     for c in range(CL):
         third = pltpu.roll(tiles[16], TILE - 16 * c, 1) if c else tiles[16]
@@ -335,6 +348,11 @@
         rest = (noise - top.astype(F32)).astype(BF)
         both = dot(jnp.concatenate([top, rest], axis=0), order)
         out_ref[c] = stack_ref[c].astype(F32) - (both[0:MB] + both[MB:])
+        copy = pltpu.make_async_copy(out_ref.at[c], out_hbm.at[c], sems.at[c])
+        copy.start()
+        copies.append(copy)
+    for copy in copies:
+        copy.wait()
 
 
 def call(kernel, outs, scratch=(), smem=0, n=0, loose=0, name=None, limit=20, where=None):
@@ -358,14 +376,22 @@
     return pltpu.VMEM(dims, dtype)
 
 
+def far(x):
+    return pltpu.with_memory_space_constraint(x, pltpu.HBM)
+
+
 def near(x):
     return pltpu.with_memory_space_constraint(x, pltpu.VMEM)
 
 
 def build_send(dest, cell, traces):
-    outs = (jax.ShapeDtypeStruct((OWNERS, PAY, TS), BF), jax.ShapeDtypeStruct((8, 128), F32))
-    scratch = [pltpu.VMEM((OWNERS, PAY, TS), BF), pltpu.SemaphoreType.DMA((4,))]
-    return call(send_kernel, outs, scratch, n=3, name="send", where=(pl.ANY, pltpu.VMEM))(dest, cell, traces)
+    outs = (jax.ShapeDtypeStruct((OWNERS, PAY, TILE), BF), jax.ShapeDtypeStruct((8, 128), F32))
+    scratch = [pltpu.VMEM((OWNERS, PAY, TILE), BF), pltpu.SemaphoreType.DMA((4,))]
+    scratch += [pltpu.VMEM((1, COUNT), jnp.int32), pltpu.VMEM((1, COUNT), jnp.int32), pltpu.VMEM((COUNT, TS), BF)]
+    scratch += [pltpu.SemaphoreType.DMA((3,))]
+    return call(send_kernel, outs, scratch, loose=3, name="send", where=(pl.ANY, pltpu.VMEM))(
+        far(dest), far(cell), far(traces)
+    )
 
 
 def build_weights(w_first, w_mid, w_last, bias, token):
@@ -385,6 +411,8 @@
 
 def convolve(pos, core, low, high, stack, weights):
     scratch = [
+        pltpu.VMEM((CL, MB, TS), F32),
+        pltpu.SemaphoreType.DMA((CL,)),
         pltpu.VMEM((80, 20 * TILE), BF),
         pltpu.VMEM((80 * CH, EXT), BF),
         pltpu.VMEM((R2 * CH, EXT), BF),
@@ -392,7 +420,7 @@
         pltpu.VMEM((3, MB, 20 * TILE), F32),
         pltpu.VMEM((3, CH, WIDE), BF),
     ]
-    return call(conv_kernel, jax.ShapeDtypeStruct((CL, MB, TS), F32), scratch, smem=1, n=8, name="conv", limit=40)(
+    return call(conv_kernel, jax.ShapeDtypeStruct((CL, MB, TS), F32), scratch, smem=1, n=8, name="conv", limit=40, where=(pl.ANY,))(
         pos, near(core), near(low), near(high), near(stack), *[near(w) for w in weights]
     )
 

time: 67.3 us -> 65.1 us (0.967)
  local copies, waits for them, and re-layouts: 2.44 us -> 0.03 us
  Pallas kernels: 21.2 us -> 21.9 us
  waiting for transfers between devices: 23.4 us -> 22.7 us
    unnamed x14 -> x8, local copies, waits for them, and re-layouts: 2.44 us -> 0.03 us
    pallas_call x1, Pallas kernels: 3.33 us -> 4.22 us  [build_send(): call(send_kernel, outs, scratch, loose=3, name='send', where=(pl.ANY, plt...]
    all_to_all x1, waiting for transfers between devices: 17.1 us -> 16.4 us  [shards(): lax.all_to_all(send, ('offset', 'mid'), split_axis=0, concat_axis=0, tile...]
where the time goes in v1:
time: 65.1 us; the launch traced here: 64.7 us
  waiting for transfers between devices  22.7 us (35%)
  Pallas kernels  21.9 us (34%)
  starting transfers between devices  19.7 us (30%)
    all_to_all x1, waiting for transfers between devices, shards(): lax.all_to_all(send, ('offset', 'mid'), split_axis=0, concat_axis=0, tile...  16.4 us
    pallas_call x1, Pallas kernels, convolve(): call(conv_kernel, jax.ShapeDtypeStruct((CL, MB, TS), F32), scratch, smem=...  14.7 us
    all_to_all x1, starting transfers between devices, shards(): lax.all_to_all(send, ('offset', 'mid'), split_axis=0, concat_axis=0, tile...  9.56 us
    ppermute x2, starting transfers between devices, neighbours(): lax.ppermute(high_edge, axis, up)  6.72 us
    ppermute x2, waiting for transfers between devices, neighbours(): lax.ppermute(low_edge, axis, down)  6.31 us
    pallas_call x1, Pallas kernels, build_send(): call(send_kernel, outs, scratch, loose=3, name='send', where=(pl.ANY, plt...  4.22 us
    ppermute x2, starting transfers between devices, neighbours(): lax.ppermute(low_edge, axis, down)  3.39 us
  transfers between devices with their start and end apart: 5, of which 3 were waited for; matrix products, arithmetic and copies ran while one was open for 0% of the time, Pallas kernels for 2%

profile of v1, /device:TPU:1, one launch (start us, length us, event | category | flops | bytes accessed | tf_op | source)
XLA Modules:
  0.0 64.7 jit_solution(8877379079390239749)
XLA Ops:
  0.0 4.2 %send.1 = (bf16[32,136,128]{2,1,0:T(8,128)(2,1)}, f32[8,128]{1,0:T(8,128)S(1)}) custom-call(s32[1,1024]{1,0:T(1,128)} %bitcast.4, s32[1,1024]{1,0:T(1,128)} %bitcast.5, bf16[1024,256]{1,0:T(8,128)(2,1)} %traces_hbm.1), custom_call_target="tpu_custom_call" | custom-call | tf_op jit(solution)/shard_map/send/pallas_call | solution.py:392
  4.2 0.0 copy-start
  4.2 0.0 copy-start.1
  4.3 0.0 copy-start.2
  4.3 0.0 copy-start.3
  4.3 9.6 %all-to-all-start = ((bf16[32,136,128]{2,1,0:T(8,128)(2,1)}), bf16[32,136,128]{2,1,0:T(8,128)(2,1)S(1)}, u32[]{:S(2)}, u32[]{:S(2)}) async-start(bf16[32,136,128]{2,1,0:T(8,128)(2,1)} %get-tuple-element.17), calls=%async_computation | async-start | bytes 2228224 | tf_op jit(solution)/shard_map/all_to_all | solution.py:437
  13.9 0.0 copy-done
  13.9 0.0 copy-done.1
  13.9 0.0 copy-done.2
  13.9 0.0 copy-done.3
  13.9 1.1 %weights.1 = (bf16[1248,256]{1,0:T(8,128)(2,1)S(1)}, bf16[48,256]{1,0:T(8,128)(2,1)S(1)}, bf16[48,256]{1,0:T(8,128)(2,1)S(1)}, bf16[24,160]{1,0:T(8,128)(2,1)S(1)}) custom-call(bf16[16,9]{1,0:T(8,128)(2,1)S(1)} %copy-done.1, bf16[2,16,144]{2,1,0:T(8,128)(2,1)S(1)} %copy-done, bf16[1,144]{1,0:T(2,128)(2,1)S(1)} %copy-done.3, f32[3,16]{1,0:T(4,128)S(1)} %copy-done.2, ...), custom_call_target="tpu_custom_call" | custom-call | tf_op jit(solution)/shard_map/weights/pallas_call | solution.py:399
  15.0 0.1 pad_add_fusion.pos_ref
  15.1 16.4 %all-to-all-done.recv_ref = bf16[32,136,128]{2,1,0:T(8,128)(2,1)S(1)} async-done(((bf16[32,136,128]{2,1,0:T(8,128)(2,1)}), bf16[32,136,128]{2,1,0:T(8,128)(2,1)S(1)}, u32[]{:S(2)}, u32[]{:S(2)}) %all-to-all-start) | async-done | bytes 1114144 | tf_op jit(solution)/shard_map/all_to_all | solution.py:437
  31.5 1.3 %stack.13 = (bf16[8,64,256]{2,1,0:T(8,128)(2,1)S(1)}, bf16[64,64]{1,0:T(8,128)(2,1)S(1)}, bf16[64,64]{1,0:T(8,128)(2,1)S(1)}) custom-call(bf16[32,136,128]{2,1,0:T(8,128)(2,1)S(1)} %all-to-all-done.recv_ref, bf16[1248,256]{1,0:T(8,128)(2,1)S(1)} %get-tuple-element.19.w1_ref, s32[2]{0:T(128)S(1)} %pad_add_fusion.pos_ref), custom_call_target="tpu_custom_call" | custom-call | tf_op jit(solution)/shard_map/stack/pallas_call | solution.py:404
  32.8 3.2 %collective-permute-start = (bf16[64,64]{1,0:T(8,128)(2,1)S(1)}, bf16[64,64]{1,0:T(8,128)(2,1)S(1)}, u32[]{:S(2)}, u32[]{:S(2)}) collective-permute-start(bf16[64,64]{1,0:T(8,128)(2,1)S(1)} %get-tuple-element.21), channel_id=1, source_target_pairs={{0,1},{1,2},{2,3},{4,5},{5,6},{6,7},{8,9},{9,10},{10,11},{12,13},{... | collective-permute-start | bytes 24584 | tf_op jit(solution)/shard_map/ppermute | solution.py:432
  36.0 1.3 %collective-permute-start.1 = (bf16[64,64]{1,0:T(8,128)(2,1)S(1)}, bf16[64,64]{1,0:T(8,128)(2,1)S(1)}, u32[]{:S(2)}, u32[]{:S(2)}) collective-permute-start(bf16[64,64]{1,0:T(8,128)(2,1)S(1)} %get-tuple-element.22), channel_id=1, source_target_pairs={{1,0},{2,1},{3,2},{5,4},{6,5},{7,6},{9,8},{10,9},{11,10},{13,12},{... | collective-permute-start | bytes 24584 | tf_op jit(solution)/shard_map/ppermute | solution.py:432
  37.3 0.0 collective-permute-done.low_ref
  37.3 3.2 %collective-permute-done.1.high_ref = bf16[64,64]{1,0:T(8,128)(2,1)S(1)} collective-permute-done((bf16[64,64]{1,0:T(8,128)(2,1)S(1)}, bf16[64,64]{1,0:T(8,128)(2,1)S(1)}, u32[]{:S(2)}, u32[]{:S(2)}) %collective-permute-start.1) | collective-permute-done | bytes 8224 | tf_op jit(solution)/shard_map/ppermute | solution.py:432
  40.5 0.6 reorder.1
  41.1 3.5 %collective-permute-start.2 = (bf16[8,2176]{1,0:T(8,128)(2,1)S(1)}, bf16[8,2176]{1,0:T(8,128)(2,1)S(1)}, u32[]{:S(2)}, u32[]{:S(2)}) collective-permute-start(bf16[8,2176]{1,0:T(8,128)(2,1)S(1)} %get-tuple-element.24), channel_id=1, source_target_pairs={{0,4},{4,8},{8,12},{12,16},{16,20},{20,24},{24,28},{1,5},{5,9},{9,... | collective-permute-start | bytes 104456 | tf_op jit(solution)/shard_map/ppermute | solution.py:432
  44.6 2.1 %collective-permute-start.3 = (bf16[8,2176]{1,0:T(8,128)(2,1)S(1)}, bf16[8,2176]{1,0:T(8,128)(2,1)S(1)}, u32[]{:S(2)}, u32[]{:S(2)}) collective-permute-start(bf16[8,2176]{1,0:T(8,128)(2,1)S(1)} %get-tuple-element.25), channel_id=1, source_target_pairs={{4,0},{8,4},{12,8},{16,12},{20,16},{24,20},{28,24},{5,1},{9,5},{13... | collective-permute-start | bytes 104456 | tf_op jit(solution)/shard_map/ppermute | solution.py:432
  46.7 0.0 collective-permute-done.2.low_ref
  46.8 3.1 %collective-permute-done.3.high_ref = bf16[8,2176]{1,0:T(8,128)(2,1)S(1)} collective-permute-done((bf16[8,2176]{1,0:T(8,128)(2,1)S(1)}, bf16[8,2176]{1,0:T(8,128)(2,1)S(1)}, u32[]{:S(2)}, u32[]{:S(2)}) %collective-permute-start.3) | collective-permute-done | bytes 34848 | tf_op jit(solution)/shard_map/ppermute | solution.py:432
  49.9 14.7 %conv.1 = f32[8,64,256]{2,1,0:T(8,128)} custom-call(s32[2]{0:T(128)S(1)} %pad_add_fusion.pos_ref, bf16[64,2176]{1,0:T(8,128)(2,1)S(1)} %get-tuple-element.23.core_ref, bf16[8,2176]{1,0:T(8,128)(2,1)S(1)} %collective-permute-done.2.low_ref, bf16[8,2176]{1,0:T(8,128)(2,1)S(1)} %collective-permute-done.3.high_ref, ...), custom_call_target="tpu_custom_call" | custom-call | tf_op jit(solution)/shard_map/conv/pallas_call | solution.py:423
Async XLA Ops:
  4.2 9.6 %copy-start = (bf16[2,16,144]{2,1,0:T(8,128)(2,1)S(1)}, bf16[2,16,144]{2,1,0:T(8,128)(2,1)}, u32[]{:S(2)}) copy-start(bf16[2,16,144]{2,1,0:T(8,128)(2,1)} %mid_ref.1) | copy-start | bytes 27652
  4.2 9.6 %copy-start.1 = (bf16[16,9]{1,0:T(8,128)(2,1)S(1)}, bf16[16,9]{1,0:T(8,128)(2,1)}, u32[]{:S(2)}) copy-start(bf16[16,9]{1,0:T(8,128)(2,1)} %first_ref.1) | copy-start | bytes 868
  4.3 9.6 %copy-start.2 = (f32[3,16]{1,0:T(4,128)S(1)}, f32[3,16]{1,0:T(4,128)}, u32[]{:S(2)}) copy-start(f32[3,16]{1,0:T(4,128)} %bias_ref.1) | copy-start | bytes 580
  4.3 9.6 %copy-start.3 = (bf16[1,144]{1,0:T(2,128)(2,1)S(1)}, bf16[1,144]{1,0:T(2,128)(2,1)}, u32[]{:S(2)}) copy-start(bf16[1,144]{1,0:T(2,128)(2,1)} %last_ref.1) | copy-start | bytes 868
  4.3 27.2 %all-to-all-start = ((bf16[32,136,128]{2,1,0:T(8,128)(2,1)}), bf16[32,136,128]{2,1,0:T(8,128)(2,1)S(1)}, u32[]{:S(2)}, u32[]{:S(2)}) async-start(bf16[32,136,128]{2,1,0:T(8,128)(2,1)} %get-tuple-element.17), calls=%async_computation | async-start | bytes 2228224 | tf_op jit(solution)/shard_map/all_to_all | solution.py:437
  32.8 4.5 %collective-permute-start = (bf16[64,64]{1,0:T(8,128)(2,1)S(1)}, bf16[64,64]{1,0:T(8,128)(2,1)S(1)}, u32[]{:S(2)}, u32[]{:S(2)}) collective-permute-start(bf16[64,64]{1,0:T(8,128)(2,1)S(1)} %get-tuple-element.21), channel_id=1, source_target_pairs={{0,1},{1,2},{2,3},{4,5},{5,6},{6,7},{8,9},{9,10},{10,11},{12,13},{... | collective-permute-start | bytes 24584 | tf_op jit(solution)/shard_map/ppermute | solution.py:432
  36.0 4.5 %collective-permute-start.1 = (bf16[64,64]{1,0:T(8,128)(2,1)S(1)}, bf16[64,64]{1,0:T(8,128)(2,1)S(1)}, u32[]{:S(2)}, u32[]{:S(2)}) collective-permute-start(bf16[64,64]{1,0:T(8,128)(2,1)S(1)} %get-tuple-element.22), channel_id=1, source_target_pairs={{1,0},{2,1},{3,2},{5,4},{6,5},{7,6},{9,8},{10,9},{11,10},{13,12},{... | collective-permute-start | bytes 24584 | tf_op jit(solution)/shard_map/ppermute | solution.py:432
  41.1 5.6 %collective-permute-start.2 = (bf16[8,2176]{1,0:T(8,128)(2,1)S(1)}, bf16[8,2176]{1,0:T(8,128)(2,1)S(1)}, u32[]{:S(2)}, u32[]{:S(2)}) collective-permute-start(bf16[8,2176]{1,0:T(8,128)(2,1)S(1)} %get-tuple-element.24), channel_id=1, source_target_pairs={{0,4},{4,8},{8,12},{12,16},{16,20},{20,24},{24,28},{1,5},{5,9},{9,... | collective-permute-start | bytes 104456 | tf_op jit(solution)/shard_map/ppermute | solution.py:432
  44.6 5.3 %collective-permute-start.3 = (bf16[8,2176]{1,0:T(8,128)(2,1)S(1)}, bf16[8,2176]{1,0:T(8,128)(2,1)S(1)}, u32[]{:S(2)}, u32[]{:S(2)}) collective-permute-start(bf16[8,2176]{1,0:T(8,128)(2,1)S(1)} %get-tuple-element.25), channel_id=1, source_target_pairs={{4,0},{8,4},{12,8},{16,12},{20,16},{24,20},{28,24},{5,1},{9,5},{13... | collective-permute-start | bytes 104456 | tf_op jit(solution)/shard_map/ppermute | solution.py:432

commit v2 on v1

--- a/solution.py
+++ b/solution.py
@@ -41,6 +41,8 @@
 ORDER1 = slots_of(R1, 2)
 ORDER2 = slots_of(R2, 4)
 SLOT2 = {r: s for s, r in enumerate(ORDER2)}
+INNER = [(4, 35), (43, 74)]
+EDGES = [(0, 4), (35, 43), (74, 78)]
 
 
 def iota(shape, dim):
@@ -247,66 +249,108 @@
     return pltpu.roll(block, shift % TILE, 1)
 
 
-def conv_kernel(pos_ref, core_ref, low_ref, high_ref, stack_ref, w1_ref, w2_ref, w3_ref, w4_ref, out_hbm,
-                out_ref, sems, x_ref, h1_ref, h2_ref, h3_ref, p_ref, mask_ref):
-    mid = pos_ref[0]
-    tm = pos_ref[1]
+def at(k):
+    return slice((LEAD + k) * TILE, (LEAD + k + 1) * TILE)
+
+
+CHUNKS = [(k * CHUNK, min(CHUNK, LANES - k * CHUNK)) for k in range(NCHUNK)]
+
+
+def valid(tm):
     lane = iota((CH, WIDE), 1)
     t = TILES * ((lane & 127) & 15) + (lane >> 7) - HALO + tm * TS
-    keep = jnp.where((t >= 0) & (t < 4 * TS), 1.0, 0.0)
-    mask_ref[0] = keep.astype(BF)
-    mask_ref[1] = (keep * jnp.where(mid > 0, 1.0, 0.0)).astype(BF)
-    mask_ref[2] = (keep * jnp.where(mid < 7, 1.0, 0.0)).astype(BF)
-
-    def at(k):
-        return slice((LEAD + k) * TILE, (LEAD + k + 1) * TILE)
-
-    image = jnp.concatenate([low_ref[...].astype(F32), core_ref[...].astype(F32), high_ref[...].astype(F32)], axis=0)
+    return jnp.where((t >= 0) & (t < 4 * TS), 1.0, 0.0)
+
+
+def fill(x_ref, image):
     x_ref[:, TILE : TILE + LANES] = image.astype(BF)
     x_ref[:, 0:TILE] = pltpu.roll(image[:, 16 * TILE :], 1, 1).astype(BF)
     for k in range(2):
         x_ref[:, (18 + k) * TILE : (19 + k) * TILE] = pltpu.roll(image[:, k * TILE : (k + 1) * TILE], TILE - 1, 1).astype(BF)
-    ones = jnp.ones((KDIM - TAPS, CHUNK), BF)
-    chunks = [(k * CHUNK, min(CHUNK, LANES - k * CHUNK)) for k in range(NCHUNK)]
+
+
+def finish(acc, row, base, wide, into_ref, slot, lead, mask_ref):
+    which = 1 if row < 0 else (2 if row >= MB else 0)
+    g = gelu_half(acc).astype(BF) * mask_ref[which, :, base : base + wide]
+    into_ref[slot * CH : (slot + 1) * CH, base + lead * TILE : base + lead * TILE + wide] = g
+
+
+def layer1(base, wide, x_ref, w1_ref, into_ref, mask_ref, runs):
+    x = [x_ref[:, base + b * TILE : base + b * TILE + wide] for b in range(3)]
+    x = jnp.concatenate(x + [jnp.ones((KDIM - TAPS, wide), BF)], axis=0)
+    for low, high in runs:
+        for s0 in range(low, high, 11):
+            count = min(11, high - s0)
+            acc = dot(w1_ref[s0 * CH : (s0 + count) * CH, :], x)
+            for j in range(count):
+                row = ORDER1[s0 + j] - 7
+                finish(acc[j * CH : (j + 1) * CH], row, base, wide, into_ref, s0 + j, LEAD, mask_ref)
+
+
+def carry(ref, runs, width):
+    for low, high in runs:
+        rows = slice(low * CH, high * CH)
+        for k in range(width):
+            ref[rows, at(TILES + k)] = turned(ref[rows, at(k)], -1)
+            ref[rows, at(-1 - k)] = turned(ref[rows, at(TILES - 1 - k)], 1)
+
+
+def inner_kernel(pos_ref, core_ref, w1_ref, h1_ref, x_ref, mask_ref):
+    mask_ref[0] = valid(pos_ref[1]).astype(BF)
+    blank = jnp.zeros((HALO, LANES), F32)
+    fill(x_ref, jnp.concatenate([blank, core_ref[...].astype(F32), blank], axis=0))
+    for base, wide in CHUNKS:
+        layer1(base, wide, x_ref, w1_ref, h1_ref, mask_ref, INNER)
+    carry(h1_ref, INNER, 2)
+
+
+def conv_kernel(pos_ref, core_ref, low_ref, high_ref, inner_ref, stack_ref, w1_ref, w2_ref, w3_ref, w4_ref, out_hbm,
+                out_ref, sems, x_ref, h1_ref, h2_ref, h3_ref, p_ref, mask_ref):
+    mid = pos_ref[0]
+    keep = valid(pos_ref[1])
+    mask_ref[0] = keep.astype(BF)
+    mask_ref[1] = (keep * jnp.where(mid > 0, 1.0, 0.0)).astype(BF)
+    mask_ref[2] = (keep * jnp.where(mid < 7, 1.0, 0.0)).astype(BF)
+    fill(x_ref, jnp.concatenate([low_ref[...].astype(F32), core_ref[...].astype(F32), high_ref[...].astype(F32)], axis=0))
+    chunks = CHUNKS
     h1_ref[R1 * CH :, :] = jnp.zeros((2 * CH, EXT), BF)
-    h1_ref[:, (LEAD + 19) * TILE :] = jnp.zeros((80 * CH, 3 * TILE), BF)
-    h2_ref[:, (LEAD + 21) * TILE :] = jnp.zeros((R2 * CH, TILE), BF)
-
-    def finish(acc, row, base, wide, into_ref, slot, lead):
-        which = 1 if row < 0 else (2 if row >= MB else 0)
-        g = gelu_half(acc).astype(BF) * mask_ref[which, :, base : base + wide]
-        into_ref[slot * CH : (slot + 1) * CH, base + lead * TILE : base + lead * TILE + wide] = g
-
-    def layer1(base, wide):
-        x = [x_ref[:, base + b * TILE : base + b * TILE + wide] for b in range(3)]
-        x = jnp.concatenate(x + [ones[:, :wide]], axis=0)
-        for s0 in range(0, R1, 13):
-            acc = dot(w1_ref[s0 * CH : (s0 + 13) * CH, :], x)
-            for j in range(13):
-                finish(acc[j * CH : (j + 1) * CH], ORDER1[s0 + j] - 7, base, wide, h1_ref, s0 + j, LEAD)
-
-    def window(ref, s0, base, wide, d):
+
+    def rows1(s0, lanes):
+        pieces, slot = [], s0
+        while slot < s0 + 5:
+            inside = any(low <= slot < high for low, high in INNER)
+            stop = slot
+            while stop < s0 + 5 and any(low <= stop < high for low, high in INNER) == inside:
+                stop += 1
+            pieces.append((inner_ref if inside else h1_ref)[slot * CH : stop * CH, lanes])
+            slot = stop
+        return pieces
+
+    def rows2(s0, lanes):
+        return [h2_ref[s0 * CH : (s0 + 5) * CH, lanes]]
+
+    def window(rows, s0, base, wide, d):
         taps = []
         for b in range(3):
             lane = base + (LEAD + (b - 1) * d) * TILE
-            taps.append(ref[s0 * CH : (s0 + 5) * CH, lane : lane + wide])
-        return jnp.concatenate(taps + [ones[:, :wide]], axis=0)
+            taps += rows(s0, slice(lane, lane + wide))
+        return jnp.concatenate(taps + [jnp.ones((KDIM - TAPS, wide), BF)], axis=0)
 
     def layer2(base, wide):
         for s0 in range(0, R1 - 2, GROUP):
-            acc = dot(w2_ref[...], window(h1_ref, s0, base, wide, 2))
+            acc = dot(w2_ref[...], window(rows1, s0, base, wide, 2))
             for j in range(GROUP):
                 if s0 + j < R1 and ORDER1[s0 + j] < R2:
                     q = ORDER1[s0 + j]
-                    finish(acc[j * CH : (j + 1) * CH], q - 5, base, wide, h2_ref, SLOT2[q], LEAD)
+                    finish(acc[j * CH : (j + 1) * CH], q - 5, base, wide, h2_ref, SLOT2[q], LEAD, mask_ref)
 
     def layer3(base, wide):
         for s0 in range(0, R2 - 2, GROUP):
-            acc = dot(w3_ref[...], window(h2_ref, s0, base, wide, 4))
+            acc = dot(w3_ref[...], window(rows2, s0, base, wide, 4))
             for j in range(GROUP):
                 if ORDER2[s0 + j] < R3:
                     q = ORDER2[s0 + j]
-                    finish(acc[j * CH : (j + 1) * CH], q - 1, base, wide, h3_ref, q, 0)
+                    finish(acc[j * CH : (j + 1) * CH], q - 1, base, wide, h3_ref, q, 0, mask_ref)
 
     def layer4(base, wide):
         for q in range(0, MB, 8):
@@ -314,17 +358,12 @@
             for b in range(3):
                 p_ref[b, q : q + 8, base + TILE : base + TILE + wide] = acc[8 * b : 8 * b + 8]
 
-    def carry(ref, rows, width):
-        for k in range(width):
-            ref[:rows, at(TILES + k)] = turned(ref[:rows, at(k)], -1)
-            ref[:rows, at(-1 - k)] = turned(ref[:rows, at(TILES - 1 - k)], 1)
-
     for n in range(NCHUNK):
-        layer1(*chunks[n])
-    carry(h1_ref, R1 * CH, 2)
+        layer1(*chunks[n], x_ref, w1_ref, h1_ref, mask_ref, EDGES)
+    carry(h1_ref, EDGES, 2)
     for n in (1, 2, 3, 4, 5, 6, 7, 8, 0):
         layer2(*chunks[n])
-    carry(h2_ref, R2 * CH, 4)
+    carry(h2_ref, [(0, R2)], 4)
     for n in (3, 4, 5, 6, 7, 8, 0, 1, 2):
         layer3(*chunks[n])
         layer4(*chunks[n])
@@ -409,7 +448,12 @@
     return call(swap_kernel, outs, n=3, name="reorder")(near(stack), near(low), near(high))
 
 
-def convolve(pos, core, low, high, stack, weights):
+def inside(pos, core, w1):
+    scratch = [pltpu.VMEM((80, 20 * TILE), BF), pltpu.VMEM((3, CH, WIDE), BF)]
+    return call(inner_kernel, shape(R1 * CH, EXT), scratch, smem=1, n=2, name="inner")(pos, near(core), near(w1))
+
+
+def convolve(pos, core, low, high, inner, stack, weights):
     scratch = [
         pltpu.VMEM((CL, MB, TS), F32),
         pltpu.SemaphoreType.DMA((CL,)),
@@ -420,8 +464,8 @@
         pltpu.VMEM((3, MB, 20 * TILE), F32),
         pltpu.VMEM((3, CH, WIDE), BF),
     ]
-    return call(conv_kernel, jax.ShapeDtypeStruct((CL, MB, TS), F32), scratch, smem=1, n=8, name="conv", limit=40, where=(pl.ANY,))(
-        pos, near(core), near(low), near(high), near(stack), *[near(w) for w in weights]
+    return call(conv_kernel, jax.ShapeDtypeStruct((CL, MB, TS), F32), scratch, smem=1, n=9, name="conv", limit=40, where=(pl.ANY,))(
+        pos, near(core), near(low), near(high), near(inner), near(stack), *[near(w) for w in weights]
     )
 
 
@@ -441,7 +485,8 @@
     low, high = neighbours(left, right, "tm")
     core, first, last = reorder(stack, low, high)
     below, above = neighbours(first, last, "mid")
-    return convolve(pos, core, below, above, stack, weights)
+    inner = inside(pos, core, weights[0])
+    return convolve(pos, core, below, above, inner, stack, weights)
 
 
 def solution(mesh):

time: 65.1 us -> 64.2 us (0.986)
  waiting for transfers between devices: 22.7 us -> 19.6 us
  Pallas kernels: 21.9 us -> 24.2 us
    pallas_call x0 -> x1, Pallas kernels: none -> 3.66 us  [inside(): call(inner_kernel, shape(R1 * CH, EXT), scratch, smem=1, n=2, name='inner')]
    ppermute x2, waiting for transfers between devices: 6.31 us -> 3.18 us  [neighbours(): lax.ppermute(low_edge, axis, down)]
    pallas_call x1, Pallas kernels: 14.7 us -> 13.3 us  [convolve(): call(conv_kernel, jax.ShapeDtypeStruct((CL, MB, TS), F32), scratch, smem=...]
  transfers between devices with their start and end apart: 5 -> 5, of which waited for: 3 -> 2; matrix products, arithmetic and copies ran while one was open for 0% -> 0% of each run, Pallas kernels for 2% -> 7%
where the time goes in v2:
time: 64.2 us; the launch traced here: 63.9 us
  Pallas kernels  24.2 us (38%)
  starting transfers between devices  19.7 us (31%)
  waiting for transfers between devices  19.6 us (31%)
    all_to_all x1, waiting for transfers between devices, shards(): lax.all_to_all(send, ('offset', 'mid'), split_axis=0, concat_axis=0, tile...  16.4 us
    pallas_call x1, Pallas kernels, convolve(): call(conv_kernel, jax.ShapeDtypeStruct((CL, MB, TS), F32), scratch, smem=...  13.3 us
    all_to_all x1, starting transfers between devices, shards(): lax.all_to_all(send, ('offset', 'mid'), split_axis=0, concat_axis=0, tile...  9.56 us
    ppermute x2, starting transfers between devices, neighbours(): lax.ppermute(high_edge, axis, up)  6.72 us
    pallas_call x1, Pallas kernels, build_send(): call(send_kernel, outs, scratch, loose=3, name='send', where=(pl.ANY, plt...  4.22 us
    pallas_call x1, Pallas kernels, inside(): call(inner_kernel, shape(R1 * CH, EXT), scratch, smem=1, n=2, name='inner')  3.66 us
    ppermute x2, starting transfers between devices, neighbours(): lax.ppermute(low_edge, axis, down)  3.39 us
    ppermute x2, waiting for transfers between devices, neighbours(): lax.ppermute(low_edge, axis, down)  3.18 us
  transfers between devices with their start and end apart: 5, of which 2 were waited for; matrix products, arithmetic and copies ran while one was open for 0% of the time, Pallas kernels for 7%

profile of v2, /device:TPU:1, one launch (start us, length us, event | category | flops | bytes accessed | tf_op | source)
XLA Modules:
  0.0 63.9 jit_solution(7577361579785223903)
XLA Ops:
  0.0 4.2 %send.1 = (bf16[32,136,128]{2,1,0:T(8,128)(2,1)}, f32[8,128]{1,0:T(8,128)S(1)}) custom-call(s32[1,1024]{1,0:T(1,128)} %bitcast.4, s32[1,1024]{1,0:T(1,128)} %bitcast.5, bf16[1024,256]{1,0:T(8,128)(2,1)} %traces_hbm.1), custom_call_target="tpu_custom_call" | custom-call | tf_op jit(solution)/shard_map/send/pallas_call | solution.py:431
  4.2 0.0 copy-start
  4.2 0.0 copy-start.1
  4.3 0.0 copy-start.2
  4.3 0.0 copy-start.3
  4.3 9.6 %all-to-all-start = ((bf16[32,136,128]{2,1,0:T(8,128)(2,1)}), bf16[32,136,128]{2,1,0:T(8,128)(2,1)S(1)}, u32[]{:S(2)}, u32[]{:S(2)}) async-start(bf16[32,136,128]{2,1,0:T(8,128)(2,1)} %get-tuple-element.17), calls=%async_computation | async-start | bytes 2228224 | tf_op jit(solution)/shard_map/all_to_all | solution.py:481
  13.9 0.0 copy-done
  13.9 0.0 copy-done.1
  13.9 0.0 copy-done.2
  13.9 1.1 %weights.1 = (bf16[1248,256]{1,0:T(8,128)(2,1)S(1)}, bf16[48,256]{1,0:T(8,128)(2,1)S(1)}, bf16[48,256]{1,0:T(8,128)(2,1)S(1)}, bf16[24,160]{1,0:T(8,128)(2,1)S(1)}) custom-call(bf16[16,9]{1,0:T(8,128)(2,1)S(1)} %copy-done.1, bf16[2,16,144]{2,1,0:T(8,128)(2,1)S(1)} %copy-done, bf16[1,144]{1,0:T(2,128)(2,1)S(1)} %copy-done.3, f32[3,16]{1,0:T(4,128)S(1)} %copy-done.2, ...), custom_call_target="tpu_custom_call" | custom-call | tf_op jit(solution)/shard_map/weights/pallas_call | solution.py:438
  15.0 0.1 pad_add_fusion.pos_ref
  15.1 16.4 %all-to-all-done.recv_ref = bf16[32,136,128]{2,1,0:T(8,128)(2,1)S(1)} async-done(((bf16[32,136,128]{2,1,0:T(8,128)(2,1)}), bf16[32,136,128]{2,1,0:T(8,128)(2,1)S(1)}, u32[]{:S(2)}, u32[]{:S(2)}) %all-to-all-start) | async-done | bytes 1114144 | tf_op jit(solution)/shard_map/all_to_all | solution.py:481
  31.5 1.3 %stack.13 = (bf16[8,64,256]{2,1,0:T(8,128)(2,1)S(1)}, bf16[64,64]{1,0:T(8,128)(2,1)S(1)}, bf16[64,64]{1,0:T(8,128)(2,1)S(1)}) custom-call(bf16[32,136,128]{2,1,0:T(8,128)(2,1)S(1)} %all-to-all-done.recv_ref, bf16[1248,256]{1,0:T(8,128)(2,1)S(1)} %get-tuple-element.19.w1_ref, s32[2]{0:T(128)S(1)} %pad_add_fusion.pos_ref), custom_call_target="tpu_custom_call" | custom-call | tf_op jit(solution)/shard_map/stack/pallas_call | solution.py:443
  32.8 3.2 %collective-permute-start = (bf16[64,64]{1,0:T(8,128)(2,1)S(1)}, bf16[64,64]{1,0:T(8,128)(2,1)S(1)}, u32[]{:S(2)}, u32[]{:S(2)}) collective-permute-start(bf16[64,64]{1,0:T(8,128)(2,1)S(1)} %get-tuple-element.21), channel_id=1, source_target_pairs={{0,1},{1,2},{2,3},{4,5},{5,6},{6,7},{8,9},{9,10},{10,11},{12,13},{... | collective-permute-start | bytes 24584 | tf_op jit(solution)/shard_map/ppermute | solution.py:476
  36.0 1.3 %collective-permute-start.1 = (bf16[64,64]{1,0:T(8,128)(2,1)S(1)}, bf16[64,64]{1,0:T(8,128)(2,1)S(1)}, u32[]{:S(2)}, u32[]{:S(2)}) collective-permute-start(bf16[64,64]{1,0:T(8,128)(2,1)S(1)} %get-tuple-element.22), channel_id=1, source_target_pairs={{1,0},{2,1},{3,2},{5,4},{6,5},{7,6},{9,8},{10,9},{11,10},{13,12},{... | collective-permute-start | bytes 24584 | tf_op jit(solution)/shard_map/ppermute | solution.py:476
  37.3 0.0 collective-permute-done.low_ref
  37.3 3.2 %collective-permute-done.1.high_ref = bf16[64,64]{1,0:T(8,128)(2,1)S(1)} collective-permute-done((bf16[64,64]{1,0:T(8,128)(2,1)S(1)}, bf16[64,64]{1,0:T(8,128)(2,1)S(1)}, u32[]{:S(2)}, u32[]{:S(2)}) %collective-permute-start.1) | collective-permute-done | bytes 8224 | tf_op jit(solution)/shard_map/ppermute | solution.py:476
  40.5 0.6 reorder.1
  41.1 3.5 %collective-permute-start.2 = (bf16[8,2176]{1,0:T(8,128)(2,1)S(1)}, bf16[8,2176]{1,0:T(8,128)(2,1)S(1)}, u32[]{:S(2)}, u32[]{:S(2)}) collective-permute-start(bf16[8,2176]{1,0:T(8,128)(2,1)S(1)} %get-tuple-element.24), channel_id=1, source_target_pairs={{0,4},{4,8},{8,12},{12,16},{16,20},{20,24},{24,28},{1,5},{5,9},{9,... | collective-permute-start | bytes 104456 | tf_op jit(solution)/shard_map/ppermute | solution.py:476
  44.6 2.1 %collective-permute-start.3 = (bf16[8,2176]{1,0:T(8,128)(2,1)S(1)}, bf16[8,2176]{1,0:T(8,128)(2,1)S(1)}, u32[]{:S(2)}, u32[]{:S(2)}) collective-permute-start(bf16[8,2176]{1,0:T(8,128)(2,1)S(1)} %get-tuple-element.25), channel_id=1, source_target_pairs={{4,0},{8,4},{12,8},{16,12},{20,16},{24,20},{28,24},{5,1},{9,5},{13... | collective-permute-start | bytes 104456 | tf_op jit(solution)/shard_map/ppermute | solution.py:476
  46.7 3.7 %inner.1.inner_ref = bf16[1248,3328]{1,0:T(8,128)(2,1)S(1)} custom-call(s32[2]{0:T(128)S(1)} %pad_add_fusion.pos_ref, bf16[64,2176]{1,0:T(8,128)(2,1)S(1)} %get-tuple-element.23.core_ref, bf16[1248,256]{1,0:T(8,128)(2,1)S(1)} %get-tuple-element.19.w1_ref), custom_call_target="tpu_custom_call" | custom-call | tf_op jit(solution)/shard_map/inner/pallas_call | solution.py:453
  50.4 0.0 collective-permute-done.2.low_ref
  50.4 0.0 collective-permute-done.3.high_ref
  50.4 13.3 %conv.1 = f32[8,64,256]{2,1,0:T(8,128)} custom-call(s32[2]{0:T(128)S(1)} %pad_add_fusion.pos_ref, bf16[64,2176]{1,0:T(8,128)(2,1)S(1)} %get-tuple-element.23.core_ref, bf16[8,2176]{1,0:T(8,128)(2,1)S(1)} %collective-permute-done.2.low_ref, bf16[8,2176]{1,0:T(8,128)(2,1)S(1)} %collective-permute-done.3.high_ref, bf16[1248,3328]{1,0:T(8,128)(2,1)S(1)} %inner.1.inner_ref, ...), custom_call_target="tpu_custom_call" | custom-call | tf_op jit(solution)/shard_map/conv/pallas_call | solution.py:467
  (1 shorter events, 0.0 us)
Async XLA Ops:
  4.2 9.6 %copy-start = (bf16[2,16,144]{2,1,0:T(8,128)(2,1)S(1)}, bf16[2,16,144]{2,1,0:T(8,128)(2,1)}, u32[]{:S(2)}) copy-start(bf16[2,16,144]{2,1,0:T(8,128)(2,1)} %mid_ref.1) | copy-start | bytes 27652
  4.2 9.6 %copy-start.1 = (bf16[16,9]{1,0:T(8,128)(2,1)S(1)}, bf16[16,9]{1,0:T(8,128)(2,1)}, u32[]{:S(2)}) copy-start(bf16[16,9]{1,0:T(8,128)(2,1)} %first_ref.1) | copy-start | bytes 868
  4.3 9.6 %copy-start.2 = (f32[3,16]{1,0:T(4,128)S(1)}, f32[3,16]{1,0:T(4,128)}, u32[]{:S(2)}) copy-start(f32[3,16]{1,0:T(4,128)} %bias_ref.1) | copy-start | bytes 580
  4.3 9.6 %copy-start.3 = (bf16[1,144]{1,0:T(2,128)(2,1)S(1)}, bf16[1,144]{1,0:T(2,128)(2,1)}, u32[]{:S(2)}) copy-start(bf16[1,144]{1,0:T(2,128)(2,1)} %last_ref.1) | copy-start | bytes 868
  4.3 27.2 %all-to-all-start = ((bf16[32,136,128]{2,1,0:T(8,128)(2,1)}), bf16[32,136,128]{2,1,0:T(8,128)(2,1)S(1)}, u32[]{:S(2)}, u32[]{:S(2)}) async-start(bf16[32,136,128]{2,1,0:T(8,128)(2,1)} %get-tuple-element.17), calls=%async_computation | async-start | bytes 2228224 | tf_op jit(solution)/shard_map/all_to_all | solution.py:481
  32.8 4.5 %collective-permute-start = (bf16[64,64]{1,0:T(8,128)(2,1)S(1)}, bf16[64,64]{1,0:T(8,128)(2,1)S(1)}, u32[]{:S(2)}, u32[]{:S(2)}) collective-permute-start(bf16[64,64]{1,0:T(8,128)(2,1)S(1)} %get-tuple-element.21), channel_id=1, source_target_pairs={{0,1},{1,2},{2,3},{4,5},{5,6},{6,7},{8,9},{9,10},{10,11},{12,13},{... | collective-permute-start | bytes 24584 | tf_op jit(solution)/shard_map/ppermute | solution.py:476
  36.0 4.5 %collective-permute-start.1 = (bf16[64,64]{1,0:T(8,128)(2,1)S(1)}, bf16[64,64]{1,0:T(8,128)(2,1)S(1)}, u32[]{:S(2)}, u32[]{:S(2)}) collective-permute-start(bf16[64,64]{1,0:T(8,128)(2,1)S(1)} %get-tuple-element.22), channel_id=1, source_target_pairs={{1,0},{2,1},{3,2},{5,4},{6,5},{7,6},{9,8},{10,9},{11,10},{13,12},{... | collective-permute-start | bytes 24584 | tf_op jit(solution)/shard_map/ppermute | solution.py:476
  41.1 9.3 %collective-permute-start.2 = (bf16[8,2176]{1,0:T(8,128)(2,1)S(1)}, bf16[8,2176]{1,0:T(8,128)(2,1)S(1)}, u32[]{:S(2)}, u32[]{:S(2)}) collective-permute-start(bf16[8,2176]{1,0:T(8,128)(2,1)S(1)} %get-tuple-element.24), channel_id=1, source_target_pairs={{0,4},{4,8},{8,12},{12,16},{16,20},{20,24},{24,28},{1,5},{5,9},{9,... | collective-permute-start | bytes 104456 | tf_op jit(solution)/shard_map/ppermute | solution.py:476
  44.6 5.8 %collective-permute-start.3 = (bf16[8,2176]{1,0:T(8,128)(2,1)S(1)}, bf16[8,2176]{1,0:T(8,128)(2,1)S(1)}, u32[]{:S(2)}, u32[]{:S(2)}) collective-permute-start(bf16[8,2176]{1,0:T(8,128)(2,1)S(1)} %get-tuple-element.25), channel_id=1, source_target_pairs={{4,0},{8,4},{12,8},{16,12},{20,16},{24,20},{28,24},{5,1},{9,5},{13... | collective-permute-start | bytes 104456 | tf_op jit(solution)/shard_map/ppermute | solution.py:476

commit v3 on v2

--- a/solution.py
+++ b/solution.py
@@ -278,13 +278,13 @@
 def layer1(base, wide, x_ref, w1_ref, into_ref, mask_ref, runs):
     x = [x_ref[:, base + b * TILE : base + b * TILE + wide] for b in range(3)]
     x = jnp.concatenate(x + [jnp.ones((KDIM - TAPS, wide), BF)], axis=0)
-    for low, high in runs:
-        for s0 in range(low, high, 11):
-            count = min(11, high - s0)
-            acc = dot(w1_ref[s0 * CH : (s0 + count) * CH, :], x)
-            for j in range(count):
-                row = ORDER1[s0 + j] - 7
-                finish(acc[j * CH : (j + 1) * CH], row, base, wide, into_ref, s0 + j, LEAD, mask_ref)
+    slots = [s for low, high in runs for s in range(low, high)]
+    for first in range(0, len(slots), 16):
+        some = slots[first : first + 16]
+        w = jnp.concatenate([w1_ref[s * CH : (s + 1) * CH, :] for s in some], axis=0)
+        acc = dot(w, x)
+        for j, s in enumerate(some):
+            finish(acc[j * CH : (j + 1) * CH], ORDER1[s] - 7, base, wide, into_ref, s, LEAD, mask_ref)
 
 
 def carry(ref, runs, width):

time: 64.2 us -> 63.4 us (0.988)
  Pallas kernels: 24.2 us -> 23.4 us
    pallas_call x1, Pallas kernels: 13.3 us -> 12.5 us  [convolve(): call(conv_kernel, jax.ShapeDtypeStruct((CL, MB, TS), F32), scratch, smem=...]
  transfers between devices with their start and end apart: 5 -> 5, of which waited for: 2 -> 2; matrix products, arithmetic and copies ran while one was open for 0% -> 0% of each run, Pallas kernels for 7% -> 8%
where the time goes in v3:
time: 63.4 us; the launch traced here: 63.1 us
  Pallas kernels  23.4 us (37%)
  starting transfers between devices  19.7 us (31%)
  waiting for transfers between devices  19.6 us (31%)
    all_to_all x1, waiting for transfers between devices, shards(): lax.all_to_all(send, ('offset', 'mid'), split_axis=0, concat_axis=0, tile...  16.4 us
    pallas_call x1, Pallas kernels, convolve(): call(conv_kernel, jax.ShapeDtypeStruct((CL, MB, TS), F32), scratch, smem=...  12.5 us
    all_to_all x1, starting transfers between devices, shards(): lax.all_to_all(send, ('offset', 'mid'), split_axis=0, concat_axis=0, tile...  9.56 us
    ppermute x2, starting transfers between devices, neighbours(): lax.ppermute(high_edge, axis, up)  6.72 us
    pallas_call x1, Pallas kernels, build_send(): call(send_kernel, outs, scratch, loose=3, name='send', where=(pl.ANY, plt...  4.22 us
    pallas_call x1, Pallas kernels, inside(): call(inner_kernel, shape(R1 * CH, EXT), scratch, smem=1, n=2, name='inner')  3.63 us
    ppermute x2, starting transfers between devices, neighbours(): lax.ppermute(low_edge, axis, down)  3.39 us
    ppermute x2, waiting for transfers between devices, neighbours(): lax.ppermute(low_edge, axis, down)  3.18 us
  transfers between devices with their start and end apart: 5, of which 2 were waited for; matrix products, arithmetic and copies ran while one was open for 0% of the time, Pallas kernels for 8%

profile of v3, /device:TPU:1, one launch (start us, length us, event | category | flops | bytes accessed | tf_op | source)
XLA Modules:
  0.0 63.1 jit_solution(10628035070978703948)
XLA Ops:
  0.0 4.2 %send.1 = (bf16[32,136,128]{2,1,0:T(8,128)(2,1)}, f32[8,128]{1,0:T(8,128)S(1)}) custom-call(s32[1,1024]{1,0:T(1,128)} %bitcast.4, s32[1,1024]{1,0:T(1,128)} %bitcast.5, bf16[1024,256]{1,0:T(8,128)(2,1)} %traces_hbm.1), custom_call_target="tpu_custom_call" | custom-call | tf_op jit(solution)/shard_map/send/pallas_call | solution.py:431
  4.2 0.0 copy-start
  4.2 0.0 copy-start.1
  4.3 0.0 copy-start.2
  4.3 0.0 copy-start.3
  4.3 9.6 %all-to-all-start = ((bf16[32,136,128]{2,1,0:T(8,128)(2,1)}), bf16[32,136,128]{2,1,0:T(8,128)(2,1)S(1)}, u32[]{:S(2)}, u32[]{:S(2)}) async-start(bf16[32,136,128]{2,1,0:T(8,128)(2,1)} %get-tuple-element.17), calls=%async_computation | async-start | bytes 2228224 | tf_op jit(solution)/shard_map/all_to_all | solution.py:481
  13.9 0.0 copy-done
  13.9 0.0 copy-done.1
  13.9 0.0 copy-done.2
  13.9 1.1 %weights.1 = (bf16[1248,256]{1,0:T(8,128)(2,1)S(1)}, bf16[48,256]{1,0:T(8,128)(2,1)S(1)}, bf16[48,256]{1,0:T(8,128)(2,1)S(1)}, bf16[24,160]{1,0:T(8,128)(2,1)S(1)}) custom-call(bf16[16,9]{1,0:T(8,128)(2,1)S(1)} %copy-done.1, bf16[2,16,144]{2,1,0:T(8,128)(2,1)S(1)} %copy-done, bf16[1,144]{1,0:T(2,128)(2,1)S(1)} %copy-done.3, f32[3,16]{1,0:T(4,128)S(1)} %copy-done.2, ...), custom_call_target="tpu_custom_call" | custom-call | tf_op jit(solution)/shard_map/weights/pallas_call | solution.py:438
  15.0 0.1 pad_add_fusion.pos_ref
  15.1 16.4 %all-to-all-done.recv_ref = bf16[32,136,128]{2,1,0:T(8,128)(2,1)S(1)} async-done(((bf16[32,136,128]{2,1,0:T(8,128)(2,1)}), bf16[32,136,128]{2,1,0:T(8,128)(2,1)S(1)}, u32[]{:S(2)}, u32[]{:S(2)}) %all-to-all-start) | async-done | bytes 1114144 | tf_op jit(solution)/shard_map/all_to_all | solution.py:481
  31.5 1.3 %stack.13 = (bf16[8,64,256]{2,1,0:T(8,128)(2,1)S(1)}, bf16[64,64]{1,0:T(8,128)(2,1)S(1)}, bf16[64,64]{1,0:T(8,128)(2,1)S(1)}) custom-call(bf16[32,136,128]{2,1,0:T(8,128)(2,1)S(1)} %all-to-all-done.recv_ref, bf16[1248,256]{1,0:T(8,128)(2,1)S(1)} %get-tuple-element.19.w1_ref, s32[2]{0:T(128)S(1)} %pad_add_fusion.pos_ref), custom_call_target="tpu_custom_call" | custom-call | tf_op jit(solution)/shard_map/stack/pallas_call | solution.py:443
  32.8 3.2 %collective-permute-start = (bf16[64,64]{1,0:T(8,128)(2,1)S(1)}, bf16[64,64]{1,0:T(8,128)(2,1)S(1)}, u32[]{:S(2)}, u32[]{:S(2)}) collective-permute-start(bf16[64,64]{1,0:T(8,128)(2,1)S(1)} %get-tuple-element.21), channel_id=1, source_target_pairs={{0,1},{1,2},{2,3},{4,5},{5,6},{6,7},{8,9},{9,10},{10,11},{12,13},{... | collective-permute-start | bytes 24584 | tf_op jit(solution)/shard_map/ppermute | solution.py:476
  36.0 1.3 %collective-permute-start.1 = (bf16[64,64]{1,0:T(8,128)(2,1)S(1)}, bf16[64,64]{1,0:T(8,128)(2,1)S(1)}, u32[]{:S(2)}, u32[]{:S(2)}) collective-permute-start(bf16[64,64]{1,0:T(8,128)(2,1)S(1)} %get-tuple-element.22), channel_id=1, source_target_pairs={{1,0},{2,1},{3,2},{5,4},{6,5},{7,6},{9,8},{10,9},{11,10},{13,12},{... | collective-permute-start | bytes 24584 | tf_op jit(solution)/shard_map/ppermute | solution.py:476
  37.3 0.0 collective-permute-done.low_ref
  37.3 3.2 %collective-permute-done.1.high_ref = bf16[64,64]{1,0:T(8,128)(2,1)S(1)} collective-permute-done((bf16[64,64]{1,0:T(8,128)(2,1)S(1)}, bf16[64,64]{1,0:T(8,128)(2,1)S(1)}, u32[]{:S(2)}, u32[]{:S(2)}) %collective-permute-start.1) | collective-permute-done | bytes 8224 | tf_op jit(solution)/shard_map/ppermute | solution.py:476
  40.5 0.6 %reorder.1 = (bf16[64,2176]{1,0:T(8,128)(2,1)S(1)}, bf16[8,2176]{1,0:T(8,128)(2,1)S(1)}, bf16[8,2176]{1,0:T(8,128)(2,1)S(1)}) custom-call(bf16[8,64,256]{2,1,0:T(8,128)(2,1)S(1)} %get-tuple-element.20.stack_ref, bf16[64,64]{1,0:T(8,128)(2,1)S(1)} %collective-permute-done.low_ref, bf16[64,64]{1,0:T(8,128)(2,1)S(1)} %collective-permute-done.1.high_ref), custom_call_target="tpu_custom_call" | custom-call | tf_op jit(solution)/shard_map/reorder/pallas_call | solution.py:448
  41.1 3.5 %collective-permute-start.2 = (bf16[8,2176]{1,0:T(8,128)(2,1)S(1)}, bf16[8,2176]{1,0:T(8,128)(2,1)S(1)}, u32[]{:S(2)}, u32[]{:S(2)}) collective-permute-start(bf16[8,2176]{1,0:T(8,128)(2,1)S(1)} %get-tuple-element.24), channel_id=1, source_target_pairs={{0,4},{4,8},{8,12},{12,16},{16,20},{20,24},{24,28},{1,5},{5,9},{9,... | collective-permute-start | bytes 104456 | tf_op jit(solution)/shard_map/ppermute | solution.py:476
  44.6 2.1 %collective-permute-start.3 = (bf16[8,2176]{1,0:T(8,128)(2,1)S(1)}, bf16[8,2176]{1,0:T(8,128)(2,1)S(1)}, u32[]{:S(2)}, u32[]{:S(2)}) collective-permute-start(bf16[8,2176]{1,0:T(8,128)(2,1)S(1)} %get-tuple-element.25), channel_id=1, source_target_pairs={{4,0},{8,4},{12,8},{16,12},{20,16},{24,20},{28,24},{5,1},{9,5},{13... | collective-permute-start | bytes 104456 | tf_op jit(solution)/shard_map/ppermute | solution.py:476
  46.7 3.6 %inner.1.inner_ref = bf16[1248,3328]{1,0:T(8,128)(2,1)S(1)} custom-call(s32[2]{0:T(128)S(1)} %pad_add_fusion.pos_ref, bf16[64,2176]{1,0:T(8,128)(2,1)S(1)} %get-tuple-element.23.core_ref, bf16[1248,256]{1,0:T(8,128)(2,1)S(1)} %get-tuple-element.19.w1_ref), custom_call_target="tpu_custom_call" | custom-call | tf_op jit(solution)/shard_map/inner/pallas_call | solution.py:453
  50.4 0.0 collective-permute-done.2.low_ref
  50.4 0.0 collective-permute-done.3.high_ref
  50.4 12.5 %conv.1 = f32[8,64,256]{2,1,0:T(8,128)} custom-call(s32[2]{0:T(128)S(1)} %pad_add_fusion.pos_ref, bf16[64,2176]{1,0:T(8,128)(2,1)S(1)} %get-tuple-element.23.core_ref, bf16[8,2176]{1,0:T(8,128)(2,1)S(1)} %collective-permute-done.2.low_ref, bf16[8,2176]{1,0:T(8,128)(2,1)S(1)} %collective-permute-done.3.high_ref, bf16[1248,3328]{1,0:T(8,128)(2,1)S(1)} %inner.1.inner_ref, ...), custom_call_target="tpu_custom_call" | custom-call | tf_op jit(solution)/shard_map/conv/pallas_call | solution.py:467
  (1 shorter events, 0.0 us)
Async XLA Ops:
  4.2 9.6 %copy-start = (bf16[2,16,144]{2,1,0:T(8,128)(2,1)S(1)}, bf16[2,16,144]{2,1,0:T(8,128)(2,1)}, u32[]{:S(2)}) copy-start(bf16[2,16,144]{2,1,0:T(8,128)(2,1)} %mid_ref.1) | copy-start | bytes 27652
  4.2 9.6 %copy-start.1 = (bf16[16,9]{1,0:T(8,128)(2,1)S(1)}, bf16[16,9]{1,0:T(8,128)(2,1)}, u32[]{:S(2)}) copy-start(bf16[16,9]{1,0:T(8,128)(2,1)} %first_ref.1) | copy-start | bytes 868
  4.3 9.6 %copy-start.2 = (f32[3,16]{1,0:T(4,128)S(1)}, f32[3,16]{1,0:T(4,128)}, u32[]{:S(2)}) copy-start(f32[3,16]{1,0:T(4,128)} %bias_ref.1) | copy-start | bytes 580
  4.3 9.6 %copy-start.3 = (bf16[1,144]{1,0:T(2,128)(2,1)S(1)}, bf16[1,144]{1,0:T(2,128)(2,1)}, u32[]{:S(2)}) copy-start(bf16[1,144]{1,0:T(2,128)(2,1)} %last_ref.1) | copy-start | bytes 868
  4.3 27.2 %all-to-all-start = ((bf16[32,136,128]{2,1,0:T(8,128)(2,1)}), bf16[32,136,128]{2,1,0:T(8,128)(2,1)S(1)}, u32[]{:S(2)}, u32[]{:S(2)}) async-start(bf16[32,136,128]{2,1,0:T(8,128)(2,1)} %get-tuple-element.17), calls=%async_computation | async-start | bytes 2228224 | tf_op jit(solution)/shard_map/all_to_all | solution.py:481
  32.8 4.5 %collective-permute-start = (bf16[64,64]{1,0:T(8,128)(2,1)S(1)}, bf16[64,64]{1,0:T(8,128)(2,1)S(1)}, u32[]{:S(2)}, u32[]{:S(2)}) collective-permute-start(bf16[64,64]{1,0:T(8,128)(2,1)S(1)} %get-tuple-element.21), channel_id=1, source_target_pairs={{0,1},{1,2},{2,3},{4,5},{5,6},{6,7},{8,9},{9,10},{10,11},{12,13},{... | collective-permute-start | bytes 24584 | tf_op jit(solution)/shard_map/ppermute | solution.py:476
  36.0 4.5 %collective-permute-start.1 = (bf16[64,64]{1,0:T(8,128)(2,1)S(1)}, bf16[64,64]{1,0:T(8,128)(2,1)S(1)}, u32[]{:S(2)}, u32[]{:S(2)}) collective-permute-start(bf16[64,64]{1,0:T(8,128)(2,1)S(1)} %get-tuple-element.22), channel_id=1, source_target_pairs={{1,0},{2,1},{3,2},{5,4},{6,5},{7,6},{9,8},{10,9},{11,10},{13,12},{... | collective-permute-start | bytes 24584 | tf_op jit(solution)/shard_map/ppermute | solution.py:476
  41.1 9.3 %collective-permute-start.2 = (bf16[8,2176]{1,0:T(8,128)(2,1)S(1)}, bf16[8,2176]{1,0:T(8,128)(2,1)S(1)}, u32[]{:S(2)}, u32[]{:S(2)}) collective-permute-start(bf16[8,2176]{1,0:T(8,128)(2,1)S(1)} %get-tuple-element.24), channel_id=1, source_target_pairs={{0,4},{4,8},{8,12},{12,16},{16,20},{20,24},{24,28},{1,5},{5,9},{9,... | collective-permute-start | bytes 104456 | tf_op jit(solution)/shard_map/ppermute | solution.py:476
  44.6 5.8 %collective-permute-start.3 = (bf16[8,2176]{1,0:T(8,128)(2,1)S(1)}, bf16[8,2176]{1,0:T(8,128)(2,1)S(1)}, u32[]{:S(2)}, u32[]{:S(2)}) collective-permute-start(bf16[8,2176]{1,0:T(8,128)(2,1)S(1)} %get-tuple-element.25), channel_id=1, source_target_pairs={{4,0},{8,4},{12,8},{16,12},{20,16},{24,20},{28,24},{5,1},{9,5},{13... | collective-permute-start | bytes 104456 | tf_op jit(solution)/shard_map/ppermute | solution.py:476
